TPU v7x, 256 devices: a whole 4x4x8 slice. The times are simulated.
256 devices in a mesh: seq: 32 (over y, x, core), grp: 8 (over z).
Axes of the slice: x: 4, y: 4, z: 8, core: 2. Of those that a mesh axis runs over, the one named last changes fastest.
Arguments:
- hidden_in: bfloat16 [98304, 2048], P(('grp', 'seq')), parts along dimension 0, may hold values from -8 to 8
- norm_gain: bfloat16 [2048], replicated, may hold values from 0.099609375 to 1.8984375
- w_query: bfloat16 [2048, 2048], P('seq'), may hold values from -1 to 1
- w_key: bfloat16 [2048, 128], P('seq'), may hold values from -1 to 1
- w_value: bfloat16 [2048, 128], P('seq'), may hold values from -0.125 to 0.125
- w_out: bfloat16 [2048, 2048], P('seq'), may hold values from -0.625 to 0.625
- seg_ids: int32 [98304], P('grp'), parts along dimension 0, may hold values from 0 to 1, never falling along the last dimension, each value on 1 to 11904 neighbouring positions
- cache_slot: int32 [768], P('grp'), parts along dimension 0, may hold values from 0 to 95, each once
Outputs:
- hidden_out: bfloat16 [98304, 2048], P(('grp', 'seq')), parts along dimension 0
- kv_cache: bfloat16 [98304, 256], P(('grp', 'seq')), parts along dimension 0
There are 8 independent parts, one for each index of `grp`. A program takes and returns all parts, laid end to end along the dimension named above; an argument that names none is the same for every part. Nothing has to cross between parts.
Inputs may be any that keep to these rules, and one draw needn't show every extreme that they name: `seg_ids`: segment numbers never fall along the stream; each prompt holds 1 to 11904 tokens. `cache_slot`: every cache position appears exactly once.
All inputs are finite; a program needn't handle non-finite values.
Results may differ from a plain program's by a relative error of at most 0.01.
Values may be sent and summed in bfloat16 or wider, within the bound.
No kernel may reach another device: no remote copies, remote signals or barrier semaphores. Data moves between devices by JAX's collectives and lax.ppermute only.
A program may use at most 256 MiB of HBM per device.

v0:
```python
import jax
import jax.numpy as jnp
from jax import lax
from jax.sharding import PartitionSpec as P

WINDOW = 1024
CACHE_BLK = 128
REACH = 3


EPSILON = 1e-06


def shifted(array, axis, by):
    length = lax.axis_size(axis)
    pairs = [(i, i + by) for i in range(length) if 0 <= i + by < length]
    return lax.ppermute(array, axis, pairs)


def normalize(hidden_in, norm_gain):
    values_wide = hidden_in.astype(jnp.float32)
    mean_square = jnp.mean(values_wide * values_wide, axis=1, keepdims=True)
    return (values_wide * lax.rsqrt(mean_square + EPSILON) * norm_gain.astype(jnp.float32)).astype(
        jnp.bfloat16
    )


def attend_block(queries, key_rows, value_rows, seg_query, seg_key, pos_query, pos_key):
    row_count = queries.shape[0]
    head_dim = key_rows.shape[1]
    head_count = queries.shape[1] // head_dim
    visible = (
        (seg_query[:, None] == seg_key[None, :])
        & (pos_key[None, :] <= pos_query[:, None])
        & (pos_key[None, :] > pos_query[:, None] - WINDOW)
    )
    score_scale = 1.0 / head_dim**0.5

    def one_head(query_head):
        scores = (
            lax.dot_general(
                query_head, key_rows, (((1,), (1,)), ((), ())), preferred_element_type=jnp.float32
            )
            * score_scale
        )
        scores = jnp.where(visible, scores, -jnp.inf)
        row_top = jnp.max(scores, axis=1, keepdims=True)
        weights = jnp.exp(scores - row_top).astype(jnp.bfloat16)
        weight_sum = jnp.sum(weights.astype(jnp.float32), axis=1, keepdims=True)
        mixture = jnp.dot(weights, value_rows, preferred_element_type=jnp.float32) / weight_sum
        return mixture.astype(jnp.bfloat16)

    per_head = jnp.transpose(queries.reshape(row_count, head_count, head_dim), (1, 0, 2))
    result = lax.map(one_head, per_head)
    return jnp.transpose(result, (1, 0, 2)).reshape(row_count, head_count * head_dim)


def shards(hidden_in, norm_gain, w_query, w_key, w_value, w_out, seg_ids, cache_slot):
    row_count = hidden_in.shape[0]
    devices = lax.axis_size("seq")
    my_index = lax.axis_index("seq")
    normed = normalize(hidden_in, norm_gain)
    head_dim = w_key.shape[1]
    pieces = (
        lax.all_gather(w_query, "seq", axis=0, tiled=True),
        lax.all_gather(w_key, "seq", axis=0, tiled=True),
        lax.all_gather(w_value, "seq", axis=0, tiled=True),
    )
    columns = normed
    query_sum, key_sum, value_sum = tuple(
        (jnp.dot(columns, piece, preferred_element_type=jnp.float32) for piece in pieces)
    )
    query = query_sum.astype(jnp.bfloat16)
    stacked = jnp.concatenate(
        [key_sum.astype(jnp.bfloat16), value_sum.astype(jnp.bfloat16)], axis=1
    )
    margin = REACH * row_count
    span = (REACH + 1) * row_count
    reach_now = min(REACH, devices - 1)
    missing = jnp.zeros(((REACH - reach_now) * row_count, 2 * head_dim), jnp.bfloat16)
    received = []
    current = stacked
    for distance in range(reach_now):
        current = shifted(current, "seq", 1)
        received.append(current)
    window_rows = jnp.concatenate([missing] + received[::-1] + [stacked], axis=0)
    first_row = my_index * row_count
    seg_pad = jnp.concatenate([jnp.full((margin,), -1, jnp.int32), seg_ids])
    seg_query = lax.dynamic_slice_in_dim(seg_ids, first_row, row_count, 0)
    seg_key = lax.dynamic_slice_in_dim(seg_pad, first_row, span, 0)
    pos_query = first_row + jnp.arange(row_count, dtype=jnp.int32)
    pos_key = first_row - margin + jnp.arange(span, dtype=jnp.int32)
    attended = attend_block(
        query,
        window_rows[:, :head_dim],
        window_rows[:, head_dim:],
        seg_query,
        seg_key,
        pos_query,
        pos_key,
    )
    columns = attended
    projected = jnp.dot(
        columns,
        lax.all_gather(w_out, "seq", axis=0, tiled=True),
        preferred_element_type=jnp.float32,
    )
    hidden_out = (hidden_in.astype(jnp.float32) + projected).astype(jnp.bfloat16)
    blocks_per_dev = row_count // CACHE_BLK
    block_total = cache_slot.shape[0]
    slot_ids = jnp.arange(block_total, dtype=jnp.int32)
    source_of = jnp.sum(
        jnp.where(cache_slot[None, :] == slot_ids[:, None], slot_ids[None, :], 0), axis=1
    )
    owned_sources = lax.dynamic_slice_in_dim(
        source_of, my_index * blocks_per_dev, blocks_per_dev, 0
    )
    within = jnp.arange(row_count, dtype=jnp.int32)
    source_row = (
        jnp.repeat(owned_sources, CACHE_BLK, total_repeat_length=row_count) * CACHE_BLK
        + within % CACHE_BLK
    )
    piece = lax.all_gather(stacked, "seq", axis=0, tiled=True)
    inside = (source_row >= 0) & (source_row < piece.shape[0])
    taken = jnp.take(piece, jnp.clip(source_row, 0, piece.shape[0] - 1), axis=0)
    kv_cache = jnp.where(inside[:, None], taken, jnp.zeros_like(stacked))
    return (hidden_out, kv_cache)


def solution(mesh):
    in_specs = (
        P(("grp", "seq"), None),
        P(),
        P("seq", None),
        P("seq", None),
        P("seq", None),
        P("seq", None),
        P("grp"),
        P("grp"),
    )
    out_specs = (P(("grp", "seq"), None), P(("grp", "seq"), None))
    return jax.shard_map(shards, mesh=mesh, in_specs=in_specs, out_specs=out_specs, check_vma=False)
```

profile of v0, /device:TPU:1, one launch (start us, length us, event | category | flops | bytes accessed | tf_op | source)
XLA Modules:
  0.0 271.4 jit_solution(2322478954140555485)
XLA Ops:
  9.8 26.4 %all_gather.17 = bf16[2048,128]{1,0:T(8,128)(2,1)S(1)} all-gather(bf16[64,128]{1,0:T(8,128)(2,1)} %param.16), channel_id=1, replica_groups=mesh['seq'=32,'grp'=8] {'seq'}, dimensions={0}, use_global_device_ids=true | all-gather | bytes 540672 | tf_op jit(solution)/shard_map/all_gather | solution.py:67
  36.3 24.1 %all_gather.16 = bf16[2048,128]{1,0:T(8,128)(2,1)S(1)} all-gather(bf16[64,128]{1,0:T(8,128)(2,1)} %param.15), channel_id=1, replica_groups=mesh['seq'=32,'grp'=8] {'seq'}, dimensions={0}, use_global_device_ids=true | all-gather | bytes 540672 | tf_op jit(solution)/shard_map/all_gather | solution.py:66
  63.4 1.9 collective-permute-start
  66.3 2.0 fusion.23
  68.4 4.1 %collective-permute-start.1 = (bf16[384,256]{0,1:T(8,128)(2,1)S(1)}, bf16[384,256]{0,1:T(8,128)(2,1)S(1)}, u32[]{:S(2)}, u32[]{:S(2)}) collective-permute-start(bf16[384,256]{0,1:T(8,128)(2,1)S(1)} %collective-permute-done), channel_id=1, source_target_pairs={{0,8},{8,16},{16,24},{24,32},{32,40},{40,48},{48,56},{56,64},{64,7... | collective-permute-start | bytes 589832 | tf_op jit(solution)/shard_map/ppermute | solution.py:17
  72.5 2.6 collective-permute-done.1
  75.1 4.6 %collective-permute-start.2 = (bf16[384,256]{0,1:T(8,128)(2,1)S(1)}, bf16[384,256]{0,1:T(8,128)(2,1)S(1)}, u32[]{:S(2)}, u32[]{:S(2)}) collective-permute-start(bf16[384,256]{0,1:T(8,128)(2,1)S(1)} %collective-permute-done.1), channel_id=1, source_target_pairs={{0,8},{8,16},{16,24},{24,32},{32,40},{40,48},{48,56},{56,64},{64,7... | collective-permute-start | bytes 589832 | tf_op jit(solution)/shard_map/ppermute | solution.py:17
  79.7 3.3 %collective-permute-done.2 = bf16[384,256]{0,1:T(8,128)(2,1)S(1)} collective-permute-done((bf16[384,256]{0,1:T(8,128)(2,1)S(1)}, bf16[384,256]{0,1:T(8,128)(2,1)S(1)}, u32[]{:S(2)}, u32[]{:S(2)}) %collective-permute-start.2) | collective-permute-done | bytes 196640 | tf_op jit(solution)/shard_map/ppermute | solution.py:17
  84.9 37.7 %all-gather.8.cloned.1.call-done = bf16[12288,256]{0,1:T(8,128)(2,1)} async-done(((bf16[384,256]{0,1:T(8,128)(2,1)}), bf16[12288,256]{0,1:T(8,128)(2,1)}) %all-gather.8.cloned.1.call-update) | async-done | bytes 6291472 | tf_op jit(solution)/shard_map/all_gather | solution.py:123
  122.7 8.6 %copy.23 = bf16[12288,256]{1,0:T(8,128)(2,1)} copy(bf16[12288,256]{0,1:T(8,128)(2,1)} %all-gather.8.cloned.1.call-done) | data formatting | bytes 12582912 | tf_op jit(solution)/shard_map/all_gather | solution.py:123
  131.3 5.3 %gather_fusion = bf16[384,256]{1,0:T(8,128)(2,1)S(1)} fusion(bf16[12288,256]{1,0:T(8,128)(2,1)} %copy.23, s32[1024]{0:T(1024)S(1)} %pad_clamp_fusion), kind=kCustom, calls=%fused_computation | custom fusion | bytes 394752 | tf_op jit(solution)/shard_map/jit(_take)/gather | solution.py:125
  137.4 45.4 %all-gather.4.cloned.1.call-done = bf16[2048,2048]{1,0:T(8,128)(2,1)} async-done(((bf16[64,2048]{1,0:T(8,128)(2,1)}), bf16[2048,2048]{1,0:T(8,128)(2,1)}) %all-gather.4.cloned.1.call-update) | async-done | bytes 8388624 | tf_op jit(solution)/shard_map/all_gather | solution.py:65
  182.8 6.8 %fusion.12 = bf16[48,16,8,128]{3,2,1,0:T(8,128)(2,1)S(1)} fusion(bf16[2048,2048]{1,0:T(8,128)(2,1)} %all-gather.4.cloned.1.call-done, bf16[384,2048]{1,0:T(8,128)(2,1)S(1)} %copy-done, f32[2048]{0:T(1024)S(1)} %convert_element_type.32, f32[384]{0:T(512)S(1)} %add_rsqrt_fusion), kind=kOutput, calls=%fused_computation.22 | convolution fusion | flops 3225157632 | bytes 11544064 | tf_op jit(solution)/shard_map/dot_general | solution.py:71
  190.1 66.2 %while.12 = (s32[]{:T(128)}, bf16[16,384,128]{1,2,0:T(8,128)(2,1)}, bf16[16,384,128]{2,1,0:T(8,128)(2,1)S(1)}, bf16[1536,128]{1,0:T(8,128)(2,1)}, bf16[1536,128]...) while((s32[]{:T(128)}, bf16[16,384,128]{1,2,0:T(8,128)(2,1)}, ...), condition=%wide.region_4.5_spmd.clone, body=%wide.region_1.4_spmd.clone.sunk | while | flops 309165312 | bytes 10055833 | solution.py:54
  194.2 1.9 fusion.47
  206.6 1.9 fusion.47
  214.9 1.9 fusion.47
  219.0 1.9 fusion.47
  223.2 1.9 fusion.47
  227.3 1.9 fusion.47
  231.5 1.9 fusion.47
  235.6 1.9 fusion.47
  239.8 1.9 fusion.47
  256.3 8.5 %fusion.11 = bf16[384,2048]{1,0:T(8,128)(2,1)} fusion(bf16[384,2048]{1,0:T(8,128)(2,1)S(1)} %copy-done, bf16[384,2048]{0,1:T(8,128)(2,1)} %bitcast.62, bf16[2048,2048]{1,0:T(8,128)(2,1)} %all-gather.6.cloned.1.call-done), kind=kOutput, calls=%fused_computation.19 | convolution fusion | flops 3223584768 | bytes 13107200 | tf_op jit(solution)/shard_map/dot_general | solution.py:103
  (140 shorter events, 58.9 us)
Async XLA Ops:
  7.2 53.2 %copy-start = (bf16[384,2048]{1,0:T(8,128)(2,1)S(1)}, bf16[384,2048]{1,0:T(8,128)(2,1)}, u32[]{:S(2)}) copy-start(bf16[384,2048]{1,0:T(8,128)(2,1)} %param.12) | copy-start | bytes 4718596
  7.2 115.5 %all-gather.8.cloned.1.call-start = ((), (), s32[]{:S(2)}) async-start(), calls=%async_computation.2 | async-start | bytes 6488064 | tf_op jit(solution)/shard_map/all_gather | solution.py:123
  61.1 4.3 %copy-start.3 = (s32[96]{0:T(128)S(1)}, s32[96]{0:T(128)}, u32[]{:S(2)}) copy-start(s32[96]{0:T(128)} %param.19) | copy-start | bytes 1156
  61.1 5.1 %copy-start.2 = (s32[12288]{0:T(1024)S(1)}, s32[12288]{0:T(1024)}, u32[]{:S(2)}) copy-start(s32[12288]{0:T(1024)} %param.18) | copy-start | bytes 147460
  62.6 120.3 %all-gather.4.cloned.1.call-start = ((), (), s32[]{:S(2)}) async-start(), calls=%async_computation | async-start | bytes 8650752 | tf_op jit(solution)/shard_map/all_gather | solution.py:65
  63.3 193.0 %all-gather.6.cloned.1.call-start = ((), (), s32[]{:S(2)}) async-start(), calls=%async_computation.1 | async-start | bytes 8650752 | tf_op jit(solution)/shard_map/all_gather | solution.py:105
  63.4 5.0 %collective-permute-start = (bf16[384,256]{0,1:T(8,128)(2,1)}, bf16[384,256]{0,1:T(8,128)(2,1)S(1)}, u32[]{:S(2)}, u32[]{:S(2)}) collective-permute-start(bf16[384,256]{0,1:T(8,128)(2,1)} %pad_maximum_fusion), channel_id=1, source_target_pairs={{0,8},{8,16},{16,24},{24,32},{32,40},{40,48},{48,56},{56,64},{64,7... | collective-permute-start | bytes 589832 | tf_op jit(solution)/shard_map/ppermute | solution.py:17
  68.4 6.7 %collective-permute-start.1 = (bf16[384,256]{0,1:T(8,128)(2,1)S(1)}, bf16[384,256]{0,1:T(8,128)(2,1)S(1)}, u32[]{:S(2)}, u32[]{:S(2)}) collective-permute-start(bf16[384,256]{0,1:T(8,128)(2,1)S(1)} %collective-permute-done), channel_id=1, source_target_pairs={{0,8},{8,16},{16,24},{24,32},{32,40},{40,48},{48,56},{56,64},{64,7... | collective-permute-start | bytes 589832 | tf_op jit(solution)/shard_map/ppermute | solution.py:17
  75.1 7.9 %collective-permute-start.2 = (bf16[384,256]{0,1:T(8,128)(2,1)S(1)}, bf16[384,256]{0,1:T(8,128)(2,1)S(1)}, u32[]{:S(2)}, u32[]{:S(2)}) collective-permute-start(bf16[384,256]{0,1:T(8,128)(2,1)S(1)} %collective-permute-done.1), channel_id=1, source_target_pairs={{0,8},{8,16},{16,24},{24,32},{32,40},{40,48},{48,56},{56,64},{64,7... | collective-permute-start | bytes 589832 | tf_op jit(solution)/shard_map/ppermute | solution.py:17
  192.0 1.0 copy-start.1
  196.1 1.0 copy-start.1
  200.2 1.0 copy-start.1
  204.4 1.0 copy-start.1
  212.6 1.0 copy-start.1
  216.7 1.0 copy-start.1
  220.9 1.0 copy-start.1
  225.1 1.0 copy-start.1
  229.2 1.0 copy-start.1
  233.4 1.0 copy-start.1
  237.5 1.0 copy-start.1
  241.7 1.0 copy-start.1
  245.8 1.0 copy-start.1
  249.9 1.0 copy-start.1
  254.1 1.0 copy-start.1
  (1 other events, 1.0 us)
Sparse Core Ops, SparseCore 0:
  62.7 59.9 all-gather.7
  125.2 57.5 all-gather.3
  185.4 57.5 all-gather.5
where the time goes:
time: 273 us; the launch traced here: 271 us
  waiting for transfers between devices  89.7 us (33%)
  matrix products  54.3 us (20%)
  blocking collectives  50.5 us (18%)
  local copies, waits for them, and re-layouts  37.7 us (14%)
  other arithmetic  14.3 us (5%)
  between operations  13.9 us (5%)
  starting transfers between devices  10.7 us (4%)
    all_gather x1, waiting for transfers between devices, shards(): lax.all_gather(w_query, 'seq', axis=0, tiled=True)  45.4 us
    all_gather x1, waiting for transfers between devices, shards(): piece = lax.all_gather(stacked, 'seq', axis=0, tiled=True)  37.7 us
    dot_general x16, matrix products, one_head(): lax.dot_general(query_head, key_rows, (((1,), (1,)), ((), ())), preferred...  30 us
    all_gather x1, blocking collectives, shards(): lax.all_gather(w_value, 'seq', axis=0, tiled=True)  26.4 us
    all_gather x1, blocking collectives, shards(): lax.all_gather(w_key, 'seq', axis=0, tiled=True)  24.1 us
    dynamic_update_slice x32, local copies, waits for them, and re-layouts, attend_block(): result = lax.map(one_head, per_head)  12.5 us
    ppermute x3, starting transfers between devices, shifted(): return lax.ppermute(array, axis, pairs)  10.5 us
    all_gather x1, local copies, waits for them, and re-layouts, shards(): piece = lax.all_gather(stacked, 'seq', axis=0, tiled=True)  8.63 us
  transfers between devices with their start and end apart: 6, of which 4 were waited for; matrix products, arithmetic and copies ran while one was open for 31% of the time, Pallas kernels for 0%

commit v1 on v0

v1 whole, which is shorter than its diff:
```python
import jax
import jax.numpy as jnp
from jax import lax
from jax.experimental import pallas as pl
from jax.experimental.pallas import tpu as pltpu
from jax.sharding import Mesh, PartitionSpec as P

WINDOW = 1024
BLK = 128
HD = 128
NY = 4
NX = 4
SEQ = ("y", "x", "core")
EPSILON = 1e-06
LOG2E = 1.4426950408889634
MASKED = -1e30
REL = (0, -1, 1, 2)


def normalize(hidden_in, norm_gain):
    wide = hidden_in.astype(jnp.float32)
    mean_square = jnp.mean(wide * wide, axis=1, keepdims=True)
    return (wide * lax.rsqrt(mean_square + EPSILON) * norm_gain.astype(jnp.float32)).astype(jnp.bfloat16)


def other_core(array):
    return lax.ppermute(array, "core", [(0, 1), (1, 0)])


def turn(array, axis, by):
    n = lax.axis_size(axis)
    return lax.ppermute(array, axis, [(i, (i + by) % n) for i in range(n)])


def hop(array, phase, by):
    pairs = []
    for y in range(NY):
        for x in range(NX):
            for core in range(2):
                along_x = (core == 0) == (phase == 1)
                ty, tx = (y, (x + by) % NX) if along_x else ((y + by) % NY, x)
                pairs.append(((y * NX + x) * 2 + core, (ty * NX + tx) * 2 + core))
    return lax.ppermute(array, SEQ, pairs)


def ring_pieces(array, phase):
    half = array.shape[0] // 2
    before = hop(array, phase, 1)
    after = hop(array, phase, -1)
    far_lo = hop(before[:half], phase, 1)
    far_hi = hop(after[half:], phase, -1)
    return [array, before, after, far_lo, far_hi]


def reorder_kernel(order_ref, src_ref, dst_ref):
    dst_ref[...] = src_ref[...]


def reorder(normed, order):
    rows, cols = normed.shape
    return pl.pallas_call(
        reorder_kernel,
        out_shape=jax.ShapeDtypeStruct(normed.shape, normed.dtype),
        grid_spec=pltpu.PrefetchScalarGridSpec(
            num_scalar_prefetch=1,
            grid=(cols // BLK,),
            in_specs=[pl.BlockSpec((rows, BLK), lambda i, order_ref: (0, order_ref[i]))],
            out_specs=pl.BlockSpec((rows, BLK), lambda i, order_ref: (0, i)),
        ),
        name="reorder",
    )(order, normed)


def project(normed_ref, piece_refs):
    start = 0
    total = None
    for piece_ref in piece_refs:
        depth = piece_ref.shape[0]
        part = jnp.dot(
            normed_ref[:, start : start + depth], piece_ref[...], preferred_element_type=jnp.float32
        )
        total = part if total is None else total + part
        start += depth
    return total


def project_kernel(normed_ref, p0, p1, p2, p3, p4, out_ref):
    out_ref[...] = project(normed_ref, (p0, p1, p2, p3, p4)).astype(jnp.bfloat16)


def project_columns(normed, pieces, width, index):
    rows = normed.shape[0]
    return pl.pallas_call(
        project_kernel,
        out_shape=jax.ShapeDtypeStruct((rows, width), jnp.bfloat16),
        grid=(1,),
        in_specs=[pl.BlockSpec(normed.shape, lambda i: (0, 0))]
        + [pl.BlockSpec((p.shape[0], width), lambda i: (0, index)) for p in pieces],
        out_specs=pl.BlockSpec((rows, width), lambda i: (0, 0)),
        name="project_columns",
    )(normed, *pieces)


def attend_kernel(normed_ref, p0, p1, p2, p3, p4, key_ref, value_ref, segq_ref, segk_ref, out_ref, q_ref, v_ref):
    rows, width = out_ref.shape
    span = WINDOW + BLK
    q_ref[...] = project(normed_ref, (p0, p1, p2, p3, p4)).astype(jnp.bfloat16)
    v_ref[:, :HD] = value_ref[...]
    v_ref[:, HD:] = jnp.ones(value_ref.shape, jnp.bfloat16)
    factor = LOG2E / HD**0.5

    def block(b, carry):
        first = pl.multiple_of(b * BLK, BLK)
        row = lax.broadcasted_iota(jnp.int32, (BLK, span), 0)
        col = lax.broadcasted_iota(jnp.int32, (BLK, span), 1)
        near = (col > row) & (col <= row + WINDOW) & (segq_ref[b] == segk_ref[b])
        bias = jnp.where(near, 0.0, MASKED)
        keys = key_ref[pl.ds(first, span), :]
        values = v_ref[pl.ds(first, span), :]
        for head in range(width // HD):
            query = q_ref[pl.ds(first, BLK), head * HD : (head + 1) * HD]
            scores = lax.dot_general(
                query, keys, (((1,), (1,)), ((), ())), preferred_element_type=jnp.float32
            )
            scores = scores * factor + bias
            top = jnp.max(scores, axis=1, keepdims=True)
            weights = jnp.exp2(scores - top).astype(jnp.bfloat16)
            mixed = jnp.dot(weights, values, preferred_element_type=jnp.float32)
            out_ref[pl.ds(first, BLK), head * HD : (head + 1) * HD] = (
                mixed[:, :HD] / mixed[:, HD:]
            ).astype(jnp.bfloat16)
        return carry

    lax.fori_loop(0, rows // BLK, block, 0)


def attend(normed, pieces, width, index, keys, values, segq, segk):
    rows = normed.shape[0]
    whole = lambda a: pl.BlockSpec(a.shape, lambda i: (0,) * a.ndim)
    return pl.pallas_call(
        attend_kernel,
        out_shape=jax.ShapeDtypeStruct((rows, width), jnp.bfloat16),
        grid=(1,),
        in_specs=[whole(normed)]
        + [pl.BlockSpec((p.shape[0], width), lambda i: (0, index)) for p in pieces]
        + [whole(keys), whole(values), whole(segq), whole(segk)],
        out_specs=pl.BlockSpec((rows, width), lambda i: (0, 0)),
        scratch_shapes=[
            pltpu.VMEM((rows, width), jnp.bfloat16),
            pltpu.VMEM((keys.shape[0], 2 * HD), jnp.bfloat16),
        ],
        name="attend",
    )(normed, *pieces, keys, values, segq, segk)


def pick_kernel(index_ref, a, b, c, d, oa, ob, oc, od):
    oa[...] = a[...]
    ob[...] = b[...]
    oc[...] = c[...]
    od[...] = d[...]


def pick_blocks(blocks, index):
    count = index.shape[1]
    shape = (1,) + blocks.shape[1:]
    spec = lambda k: pl.BlockSpec(shape, lambda i, index_ref: (index_ref[k, i], 0, 0))
    out = pl.BlockSpec(shape, lambda i, index_ref: (i, 0, 0))
    return pl.pallas_call(
        pick_kernel,
        out_shape=[jax.ShapeDtypeStruct((count,) + blocks.shape[1:], blocks.dtype)] * 4,
        grid_spec=pltpu.PrefetchScalarGridSpec(
            num_scalar_prefetch=1,
            grid=(count,),
            in_specs=[spec(k) for k in range(4)],
            out_specs=[out] * 4,
        ),
        name="pick_blocks",
    )(index, blocks, blocks, blocks, blocks)


def place(difference):
    d = difference % 4
    return jnp.where(d == 0, 0, jnp.where(d == 3, 1, jnp.where(d == 1, 2, 3)))


def shards(hidden_in, norm_gain, w_query, w_key, w_value, w_out, seg_ids, cache_slot):
    row_count, width = hidden_in.shape
    half = width // 2
    y, x, core = (lax.axis_index(a) for a in SEQ)
    first_core = core == 0
    chip = y * NX + x

    part0 = jnp.concatenate([w_query[:, :half], w_key], axis=1)
    part1 = jnp.concatenate([w_query[:, half:], w_value], axis=1)
    keep = jnp.where(first_core, part0, part1)
    taken = other_core(jnp.where(first_core, part1, part0))
    own = jnp.concatenate(
        [jnp.where(first_core, keep, taken), jnp.where(first_core, taken, keep)], axis=0
    )
    ring = jnp.concatenate(ring_pieces(own, 1), axis=0)
    pieces = ring_pieces(ring, 2)
    w_out_whole = lax.all_gather(w_out, SEQ, axis=0, tiled=True)

    outer, inner = (jnp.asarray(REL, jnp.int32)[:, None], jnp.asarray(REL, jnp.int32)[None, :])
    order_0 = ((y + outer) % NY) * NX + (x + inner) % NX
    order_1 = ((y + inner) % NY) * NX + (x + outer) % NX
    order = jnp.where(first_core, order_0, order_1).reshape(NY * NX)

    mine = normalize(hidden_in, norm_gain)
    theirs = other_core(mine)
    normed = jnp.concatenate(
        [jnp.where(first_core, mine, theirs), jnp.where(first_core, theirs, mine)], axis=0
    )
    normed = reorder(normed, order)
    chip_rows = 2 * row_count

    made = project_columns(normed, pieces, HD, half // HD)
    seq_count = NY * NX * 2
    back_1 = lax.ppermute(made, SEQ, [(i, i + 2) for i in range(seq_count - 2)])
    short = WINDOW - chip_rows
    back_2 = lax.ppermute(made[chip_rows - short :], SEQ, [(i, i + 4) for i in range(seq_count - 4)])
    window = jnp.concatenate([back_2, back_1, made], axis=0)
    swapped = other_core(window)
    keys = jnp.where(first_core, window, swapped)
    values = jnp.where(first_core, swapped, window)

    seg_pad = jnp.concatenate([jnp.full((WINDOW,), -1, jnp.int32), seg_ids])
    seg_here = lax.dynamic_slice_in_dim(seg_pad, chip * chip_rows, WINDOW + chip_rows, 0)
    blocks = chip_rows // BLK
    segq = seg_here[WINDOW:].reshape(blocks, BLK, 1)
    segk = jnp.stack([seg_here[b * BLK : b * BLK + WINDOW + BLK] for b in range(blocks)])[:, None, :]

    group = 4 * HD
    kept, got = [], []
    for index in range(half // group):
        attended = attend(normed, pieces, group, index, keys, values, segq, segk)
        low, high = attended[:row_count], attended[row_count:]
        kept.append(jnp.where(first_core, low, high))
        got.append(other_core(jnp.where(first_core, high, low)))
    kept = jnp.concatenate(kept, axis=1)
    got = jnp.concatenate(got, axis=1)
    columns = jnp.concatenate(
        [jnp.where(first_core, kept, got), jnp.where(first_core, got, kept)], axis=1
    )
    projected = jnp.dot(columns, w_out_whole, preferred_element_type=jnp.float32)
    hidden_out = (hidden_in.astype(jnp.float32) + projected).astype(jnp.bfloat16)

    made = made.reshape(blocks, BLK, HD)
    column = jnp.concatenate([made, turn(made, "y", 1), turn(made, "y", -1), turn(made, "y", 2)], axis=0)
    total = cache_slot.shape[0]
    ids = jnp.arange(total, dtype=jnp.int32)
    source_of = jnp.sum(jnp.where(cache_slot[None, :] == ids[:, None], ids[None, :], 0), axis=1)
    row_sources = lax.dynamic_slice_in_dim(source_of, y * NX * blocks, NX * blocks, 0).reshape(NX, blocks)
    source_y = row_sources // (NX * blocks)
    source_x = (row_sources // blocks) % NX
    local = place(source_y - y) * blocks + row_sources % blocks
    targets = (x + jnp.asarray((0, 1, -1, 2), jnp.int32)) % NX
    here, right, left, across = pick_blocks(column, jnp.take(local, targets, axis=0))
    arrived = [here, turn(right, "x", 1), turn(left, "x", -1), turn(across, "x", 2)]
    where_from = place(jnp.take(source_x, x, axis=0) - x)[:, None, None]
    owned = arrived[3]
    for k in (2, 1, 0):
        owned = jnp.where(where_from == k, arrived[k], owned)
    low, high = owned[: blocks // 2], owned[blocks // 2 :]
    cache_keep = jnp.where(first_core, low, high)
    cache_got = other_core(jnp.where(first_core, high, low))
    kv_cache = jnp.concatenate(
        [jnp.where(first_core, cache_keep, cache_got), jnp.where(first_core, cache_got, cache_keep)], axis=2
    ).reshape(row_count, 2 * HD)
    return (hidden_out, kv_cache)


def solution(mesh):
    grid = Mesh(mesh.devices.reshape(NY, NX, 2, mesh.devices.shape[1]), SEQ + ("grp",))
    everywhere = P(("grp",) + SEQ, None)
    in_specs = (
        everywhere,
        P(),
        P(SEQ, None),
        P(SEQ, None),
        P(SEQ, None),
        P(SEQ, None),
        P("grp"),
        P("grp"),
    )
    return jax.shard_map(
        shards, mesh=grid, in_specs=in_specs, out_specs=(everywhere, everywhere), check_vma=False
    )
```

time: 273 us -> 165 us (0.60)
  waiting for transfers between devices: 89.7 us -> 17.2 us
  blocking collectives: 50.5 us -> 0 us
  Pallas kernels: 0 us -> 46.6 us
  matrix products: 54.3 us -> 7.87 us
  starting transfers between devices: 10.7 us -> 38.1 us
  local copies, waits for them, and re-layouts: 37.7 us -> 15.1 us
  other arithmetic: 14.3 us -> 24.8 us
    all_gather x3 -> x1, waiting for transfers between devices: 83.2 us -> 0.02 us  [shards(): w_out_whole = lax.all_gather(w_out, SEQ, axis=0, tiled=True)]
    all_gather x2 -> x0, blocking collectives: 50.5 us -> none  [the longest x1 26.4 us: shards(): lax.all_gather(w_value, 'seq', axis=0, tiled=True)]
    pallas_call x0 -> x5, Pallas kernels: none -> 46.6 us  [the longest x2 27.3 us: attend(): pl.pallas_call(attend_kernel, out_shape=jax.ShapeDtypeStruct((rows, width...]
    dot_general x36 -> x1, matrix products: 54.3 us -> 7.87 us  [shards(): jnp.dot(columns, w_out_whole, preferred_element_type=jnp.float32)]
    ppermute x3 -> x22, starting transfers between devices: 10.5 us -> 38.1 us  [the longest x6 12.3 us: other_core(): return lax.ppermute(array, 'core', [(0, 1), (1, 0)])]
    dynamic_update_slice x32 -> x0, local copies, waits for them, and re-layouts: 12.5 us -> none  [attend_block(): result = lax.map(one_head, per_head)]
    ppermute x3 -> x22, waiting for transfers between devices: 5.86 us -> 16.5 us  [the longest x8 12.4 us: hop(): return lax.ppermute(array, SEQ, pairs)]
    select_n x1 -> x12, other arithmetic: 0.85 us -> 10.8 us  [the longest x1 2.44 us: shards(): jnp.where(first_core, mine, theirs)]
  transfers between devices with their start and end apart: 6 -> 23, of which waited for: 4 -> 7; matrix products, arithmetic and copies ran while one was open for 31% -> 24% of each run, Pallas kernels for 0% -> 28%
where the time goes in v1:
time: 165 us; the launch traced here: 164 us
  Pallas kernels  46.6 us (28%)
  starting transfers between devices  38.1 us (23%)
  other arithmetic  24.8 us (15%)
  waiting for transfers between devices  17.2 us (10%)
  local copies, waits for them, and re-layouts  15.1 us (9%)
  between operations  14.4 us (9%)
  matrix products  7.87 us (5%)
    pallas_call x2, Pallas kernels, attend(): pl.pallas_call(attend_kernel, out_shape=jax.ShapeDtypeStruct((rows, width...  27.3 us
    ppermute x8, waiting for transfers between devices, hop(): return lax.ppermute(array, SEQ, pairs)  12.4 us
    ppermute x6, starting transfers between devices, other_core(): return lax.ppermute(array, 'core', [(0, 1), (1, 0)])  12.3 us
    ppermute x8, starting transfers between devices, hop(): return lax.ppermute(array, SEQ, pairs)  11 us
    pallas_call x1, Pallas kernels, reorder(): pl.pallas_call(reorder_kernel, out_shape=jax.ShapeDtypeStruct(normed.shap...  10.8 us
    dot_general x1, matrix products, shards(): jnp.dot(columns, w_out_whole, preferred_element_type=jnp.float32)  7.87 us
    ppermute x1, starting transfers between devices, shards(): lax.ppermute(made[chip_rows - short:], SEQ, [(i, i + 4) for i in range(se...  6.58 us
    ppermute x6, starting transfers between devices, turn(): return lax.ppermute(array, axis, [(i, (i + by) % n) for i in range(n)])  6.53 us
  transfers between devices with their start and end apart: 23, of which 7 were waited for; matrix products, arithmetic and copies ran while one was open for 24% of the time, Pallas kernels for 28%

profile of v1, /device:TPU:1, one launch (start us, length us, event | category | flops | bytes accessed | tf_op | source)
XLA Modules:
  0.0 164.1 jit_solution(5735805129567017267)
XLA Ops:
  9.7 3.3 %collective-permute-start.1 = (bf16[64,1152]{1,0:T(8,128)(2,1)S(1)}, bf16[64,1152]{1,0:T(8,128)(2,1)S(1)}, u32[]{:S(2)}, u32[]{:S(2)}) collective-permute-start(bf16[64,1152]{1,0:T(8,128)(2,1)S(1)} %broadcast_select_fusion.12), channel_id=1, source_target_pairs={{0,8},{8,0},{1,9},{9,1},{2,10},{10,2},{3,11},{11,3},{4,12},{12,4},... | collective-permute-start | bytes 442376 | tf_op jit(solution)/shard_map/ppermute | solution.py:27
  13.7 1.8 %fusion = f32[384]{0:T(512)S(1)} fusion(bf16[384,2048]{1,0:T(8,128)(2,1)} %param.11), kind=kLoop, calls=%fused_computation.4 | loop fusion | flops 2358912 | bytes 1574400 | tf_op jit(solution)/shard_map/reduce_sum | solution.py:22
  18.7 2.7 %collective-permute-start.3 = (bf16[128,1152]{1,0:T(8,128)(2,1)S(1)}, bf16[128,1152]{1,0:T(8,128)(2,1)S(1)}, u32[]{:S(2)}, u32[]{:S(2)}) collective-permute-start(bf16[128,1152]{1,0:T(8,128)(2,1)S(1)} %pad_maximum_fusion.4), channel_id=1, source_target_pairs={{0,48},{8,200},{16,0},{24,216},{32,16},{40,232},{48,32},{56,248},{... | collective-permute-start | bytes 884744 | tf_op jit(solution)/shard_map/ppermute | solution.py:43
  21.5 4.3 %collective-permute-done.2 = bf16[128,1152]{1,0:T(8,128)(2,1)S(1)} collective-permute-done((bf16[128,1152]{1,0:T(8,128)(2,1)S(1)}, bf16[128,1152]{1,0:T(8,128)(2,1)S(1)}, u32[]{:S(2)}, u32[]{:S(2)}) %collective-permute-start.2) | collective-permute-done | bytes 294944 | tf_op jit(solution)/shard_map/ppermute | solution.py:43
  25.9 2.7 %collective-permute-start.5 = (bf16[64,1152]{1,0:T(8,128)(2,1)S(1)}, bf16[64,1152]{1,0:T(8,128)(2,1)S(1)}, u32[]{:S(2)}, u32[]{:S(2)}) collective-permute-start(bf16[64,1152]{1,0:T(8,128)(2,1)S(1)} %slice.101), channel_id=1, source_target_pairs={{0,48},{8,200},{16,0},{24,216},{32,16},{40,232},{48,32},{56,248},{... | collective-permute-start | bytes 442376 | tf_op jit(solution)/shard_map/ppermute | solution.py:43
  28.7 2.4 %collective-permute-done.4 = bf16[64,1152]{1,0:T(8,128)(2,1)S(1)} collective-permute-done((bf16[64,1152]{1,0:T(8,128)(2,1)S(1)}, bf16[64,1152]{1,0:T(8,128)(2,1)S(1)}, u32[]{:S(2)}, u32[]{:S(2)}) %collective-permute-start.4) | collective-permute-done | bytes 147488 | tf_op jit(solution)/shard_map/ppermute | solution.py:43
  31.5 2.5 %collective-permute-start.7 = (bf16[512,1152]{1,0:T(8,128)(2,1)S(1)}, bf16[512,1152]{1,0:T(8,128)(2,1)S(1)}, u32[]{:S(2)}, u32[]{:S(2)}) collective-permute-start(bf16[512,1152]{1,0:T(8,128)(2,1)S(1)} %constant_dynamic-update-slice_fusion.p0), channel_id=1, source_target_pairs={{0,192},{8,56},{16,208},{24,8},{32,224},{40,24},{48,240},{56,40},{... | collective-permute-start | bytes 3538952 | tf_op jit(solution)/shard_map/ppermute | solution.py:43
  52.1 2.7 %collective-permute-start.9 = (bf16[256,1152]{1,0:T(8,128)(2,1)}, bf16[256,1152]{1,0:T(8,128)(2,1)}, u32[]{:S(2)}, u32[]{:S(2)}) collective-permute-start(bf16[256,1152]{1,0:T(8,128)(2,1)} %slice.103), channel_id=1, source_target_pairs={{0,192},{8,56},{16,208},{24,8},{32,224},{40,24},{48,240},{56,40},{... | collective-permute-start | bytes 1769480 | tf_op jit(solution)/shard_map/ppermute | solution.py:43
  54.8 2.4 %broadcast_select_fusion.1 = (bf16[384,2048]{1,0:T(8,128)(2,1)S(1)}, bf16[384,2048]{1,0:T(8,128)(2,1)S(1)}) fusion(bf16[384,2048]{1,0:T(8,128)(2,1)} %collective-permute-done, pred[]{:T(512)S(6)} %eq.102, f32[2048]{0:T(1024)S(1)} %convert_element_type.14, f32[384]{0:T(512)S(1)} %add_rsqrt_fusion, bf16[384,2048]{1,0:T(8,128)(2,1)S(1)} %copy-done.3), kind=kLoop, calls=%fused_computation.13 | loop fusion | flops 4718592 | bytes 6301185 | tf_op jit(solution)/shard_map/jit(_where)/select_n | solution.py:212
  57.3 2.1 %pad_maximum_fusion.src_ref = bf16[768,2048]{1,0:T(8,128)(2,1)} fusion(bf16[384,2048]{1,0:T(8,128)(2,1)S(1)} %get-tuple-element.32, bf16[384,2048]{1,0:T(8,128)(2,1)S(1)} %get-tuple-element.31), kind=kLoop, calls=%fused_computation.8 | loop fusion | flops 6291456 | bytes 6291456 | tf_op jit(solution)/shard_map/concatenate | solution.py:211
  59.3 10.8 %reorder.1.normed_ref = bf16[768,2048]{1,0:T(8,128)(2,1)} custom-call(s32[16]{0:T(128)} %select_n.284.order_ref, bf16[768,2048]{1,0:T(8,128)(2,1)} %pad_maximum_fusion.src_ref), custom_call_target="tpu_custom_call" | custom-call | tf_op jit(solution)/shard_map/reorder/pallas_call | solution.py:61
  70.2 4.0 %collective-permute-done.8.p3 = bf16[256,1152]{1,0:T(8,128)(2,1)} collective-permute-done((bf16[256,1152]{1,0:T(8,128)(2,1)}, bf16[256,1152]{1,0:T(8,128)(2,1)}, u32[]{:S(2)}, u32[]{:S(2)}) %collective-permute-start.8) | collective-permute-done | bytes 589856 | tf_op jit(solution)/shard_map/ppermute | solution.py:43
  74.2 3.7 %project_columns.1 = bf16[768,128]{1,0:T(8,128)(2,1)} custom-call(bf16[768,2048]{1,0:T(8,128)(2,1)} %reorder.1.normed_ref, bf16[512,1152]{1,0:T(8,128)(2,1)} %copy-done.5, bf16[512,1152]{1,0:T(8,128)(2,1)} %copy-done, bf16[512,1152]{1,0:T(8,128)(2,1)} %copy-done.1, bf16[256,1152]{1,0:T(8,128)(2,1)} %collective-permute-done.8.p3, ...), custom_call_target="tpu_custom_call" | custom-call | tf_op jit(solution)/shard_map/project_columns/pallas_call | solution.py:93
  77.9 2.7 %collective-permute-start.16 = (bf16[6,128,128]{2,1,0:T(8,128)(2,1)}, bf16[6,128,128]{2,1,0:T(8,128)(2,1)S(1)}, u32[]{:S(2)}, u32[]{:S(2)}) collective-permute-start(bf16[6,128,128]{2,1,0:T(8,128)(2,1)} %bitcast.13), channel_id=1, source_target_pairs={{0,192},{64,0},{128,64},{192,128},{1,193},{65,1},{129,65},{193,129... | collective-permute-start | bytes 589832 | tf_op jit(solution)/shard_map/ppermute | solution.py:32
  86.2 6.6 %collective-permute-start.10 = (bf16[256,128]{1,0:T(8,128)(2,1)S(1)}, bf16[256,128]{1,0:T(8,128)(2,1)S(1)}, u32[]{:S(2)}, u32[]{:S(2)}) collective-permute-start(bf16[256,128]{1,0:T(8,128)(2,1)S(1)} %slice.104), channel_id=1, source_target_pairs={{0,32},{8,40},{16,48},{24,56},{32,64},{40,72},{48,80},{56,88},{64,... | collective-permute-start | bytes 196616 | tf_op jit(solution)/shard_map/ppermute | solution.py:221
  92.9 1.9 %pad_maximum_fusion.2.a.b.c.d = bf16[24,128,128]{2,1,0:T(8,128)(2,1)} fusion(bf16[6,128,128]{2,1,0:T(8,128)(2,1)S(1)} %collective-permute-done.17, bf16[6,128,128]{2,1,0:T(8,128)(2,1)S(1)} %collective-permute-done.16, bf16[6,128,128]{2,1,0:T(8,128)(2,1)S(1)} %collective-permute-done.15, bf16[6,128,128]{2,1,0:T(8,128)(2,1)} %bitcast.15), kind=kLoop, calls=%fused_computation.15 | loop fusion | flops 1179648 | bytes 1572864 | tf_op jit(solution)/shard_map/concatenate | solution.py:249
  94.8 4.7 %pick_blocks.1 = (bf16[6,128,128]{2,1,0:T(8,128)(2,1)}, bf16[6,128,128]{2,1,0:T(8,128)(2,1)}, bf16[6,128,128]{2,1,0:T(8,128)(2,1)}, bf16[6,128,128]{2,1,0:T(8,128)(2,1)}) custom-call(s32[4,6]{1,0:T(4,128)} %broadcast_select_fusion.18.index_ref, bf16[24,128,128]{2,1,0:T(8,128)(2,1)} %pad_maximum_fusion.2.a.b.c.d, ...), custom_call_target="tpu_custom_call" | custom-call | tf_op jit(solution)/shard_map/pick_blocks/pallas_call | solution.py:168
  99.6 2.7 %collective-permute-start.19 = (bf16[6,128,128]{2,1,0:T(8,128)(2,1)}, bf16[6,128,128]{2,1,0:T(8,128)(2,1)S(1)}, u32[]{:S(2)}, u32[]{:S(2)}) collective-permute-start(bf16[6,128,128]{2,1,0:T(8,128)(2,1)} %get-tuple-element.8), channel_id=1, source_target_pairs={{0,48},{16,0},{32,16},{48,32},{1,49},{17,1},{33,17},{49,33},{2,50}... | collective-permute-start | bytes 589832 | tf_op jit(solution)/shard_map/ppermute | solution.py:32
  102.3 4.5 %collective-permute-start.12 = (bf16[1792,128]{1,0:T(8,128)(2,1)S(1)}, bf16[1792,128]{1,0:T(8,128)(2,1)S(1)}, u32[]{:S(2)}, u32[]{:S(2)}) collective-permute-start(bf16[1792,128]{1,0:T(8,128)(2,1)S(1)} %pad_maximum_fusion.3), channel_id=1, source_target_pairs={{0,8},{8,0},{1,9},{9,1},{2,10},{10,2},{3,11},{11,3},{4,12},{12,4},... | collective-permute-start | bytes 1376264 | tf_op jit(solution)/shard_map/ppermute | solution.py:27
  107.3 3.0 %collective-permute-done.20 = bf16[6,128,128]{2,1,0:T(8,128)(2,1)S(1)} collective-permute-done((bf16[6,128,128]{2,1,0:T(8,128)(2,1)}, bf16[6,128,128]{2,1,0:T(8,128)(2,1)S(1)}, u32[]{:S(2)}, u32[]{:S(2)}) %collective-permute-start.20) | collective-permute-done | bytes 196640 | tf_op jit(solution)/shard_map/ppermute | solution.py:32
  111.3 3.8 %collective-permute-start.21 = (bf16[3,128,128]{2,1,0:T(8,128)(2,1)S(1)}, bf16[3,128,128]{2,1,0:T(8,128)(2,1)S(1)}, u32[]{:S(2)}, u32[]{:S(2)}) collective-permute-start(bf16[3,128,128]{2,1,0:T(8,128)(2,1)S(1)} %broadcast_select_fusion.16), channel_id=1, source_target_pairs={{0,8},{8,0},{1,9},{9,1},{2,10},{10,2},{3,11},{11,3},{4,12},{12,4},... | collective-permute-start | bytes 294920 | tf_op jit(solution)/shard_map/ppermute | solution.py:27
  116.3 13.6 %attend.2 = bf16[768,512]{1,0:T(8,128)(2,1)} custom-call(bf16[768,2048]{1,0:T(8,128)(2,1)} %reorder.1.normed_ref, bf16[512,1152]{1,0:T(8,128)(2,1)} %copy-done.5, bf16[512,1152]{1,0:T(8,128)(2,1)} %copy-done, bf16[512,1152]{1,0:T(8,128)(2,1)} %copy-done.1, bf16[256,1152]{1,0:T(8,128)(2,1)} %collective-permute-done.8.p3, ...), custom_call_target="tpu_custom_call" | custom-call | tf_op jit(solution)/shard_map/attend/pallas_call | solution.py:140
  131.2 13.6 %attend.3 = bf16[768,512]{1,0:T(8,128)(2,1)} custom-call(bf16[768,2048]{1,0:T(8,128)(2,1)} %reorder.1.normed_ref, bf16[512,1152]{1,0:T(8,128)(2,1)} %copy-done.5, bf16[512,1152]{1,0:T(8,128)(2,1)} %copy-done, bf16[512,1152]{1,0:T(8,128)(2,1)} %copy-done.1, bf16[256,1152]{1,0:T(8,128)(2,1)} %collective-permute-done.8.p3, ...), custom_call_target="tpu_custom_call" | custom-call | tf_op jit(solution)/shard_map/attend/pallas_call | solution.py:140
  149.4 7.9 %fusion.3 = bf16[384,2048]{1,0:T(8,128)(2,1)} fusion(bf16[384,2048]{1,0:T(8,128)(2,1)S(1)} %copy-done.4, bf16[2048,2048]{1,0:T(8,128)(2,1)} %all-gather.2.cloned.1.call-done, bf16[384,1024]{1,0:T(8,128)(2,1)S(1)} %get-tuple-element.34, bf16[384,1024]{1,0:T(8,128)(2,1)S(1)} %get-tuple-element.33), kind=kOutput, calls=%fused_computation.7 | convolution fusion | flops 3226730496 | bytes 13107200 | tf_op jit(solution)/shard_map/dot_general | solution.py:245
  (119 shorter events, 39.2 us)
Async XLA Ops:
  7.2 141.2 %all-gather.2.cloned.1.call-start = ((), (), s32[]{:S(2)}) async-start(), calls=%async_computation | async-start | bytes 8650752 | tf_op jit(solution)/shard_map/all_gather | solution.py:202
  9.7 8.8 %collective-permute-start.1 = (bf16[64,1152]{1,0:T(8,128)(2,1)S(1)}, bf16[64,1152]{1,0:T(8,128)(2,1)S(1)}, u32[]{:S(2)}, u32[]{:S(2)}) collective-permute-start(bf16[64,1152]{1,0:T(8,128)(2,1)S(1)} %broadcast_select_fusion.12), channel_id=1, source_target_pairs={{0,8},{8,0},{1,9},{9,1},{2,10},{10,2},{3,11},{11,3},{4,12},{12,4},... | collective-permute-start | bytes 442376 | tf_op jit(solution)/shard_map/ppermute | solution.py:27
  17.1 37.7 %collective-permute-start = (bf16[384,2048]{1,0:T(8,128)(2,1)}, bf16[384,2048]{1,0:T(8,128)(2,1)}, u32[]{:S(2)}, u32[]{:S(2)}) collective-permute-start(bf16[384,2048]{1,0:T(8,128)(2,1)} %fusion.2), channel_id=1, source_target_pairs={{0,8},{8,0},{1,9},{9,1},{2,10},{10,2},{3,11},{11,3},{4,12},{12,4},... | collective-permute-start | bytes 4718600 | tf_op jit(solution)/shard_map/ppermute | solution.py:27
  18.6 7.2 %collective-permute-start.2 = (bf16[128,1152]{1,0:T(8,128)(2,1)S(1)}, bf16[128,1152]{1,0:T(8,128)(2,1)S(1)}, u32[]{:S(2)}, u32[]{:S(2)}) collective-permute-start(bf16[128,1152]{1,0:T(8,128)(2,1)S(1)} %pad_maximum_fusion.4), channel_id=1, source_target_pairs={{0,16},{8,72},{16,32},{24,88},{32,48},{40,104},{48,0},{56,120},{64... | collective-permute-start | bytes 884744 | tf_op jit(solution)/shard_map/ppermute | solution.py:43
  18.7 7.2 %collective-permute-start.3 = (bf16[128,1152]{1,0:T(8,128)(2,1)S(1)}, bf16[128,1152]{1,0:T(8,128)(2,1)S(1)}, u32[]{:S(2)}, u32[]{:S(2)}) collective-permute-start(bf16[128,1152]{1,0:T(8,128)(2,1)S(1)} %pad_maximum_fusion.4), channel_id=1, source_target_pairs={{0,48},{8,200},{16,0},{24,216},{32,16},{40,232},{48,32},{56,248},{... | collective-permute-start | bytes 884744 | tf_op jit(solution)/shard_map/ppermute | solution.py:43
  25.8 5.4 %collective-permute-start.4 = (bf16[64,1152]{1,0:T(8,128)(2,1)S(1)}, bf16[64,1152]{1,0:T(8,128)(2,1)S(1)}, u32[]{:S(2)}, u32[]{:S(2)}) collective-permute-start(bf16[64,1152]{1,0:T(8,128)(2,1)S(1)} %slice.100), channel_id=1, source_target_pairs={{0,16},{8,72},{16,32},{24,88},{32,48},{40,104},{48,0},{56,120},{64... | collective-permute-start | bytes 442376 | tf_op jit(solution)/shard_map/ppermute | solution.py:43
  25.9 5.3 %collective-permute-start.5 = (bf16[64,1152]{1,0:T(8,128)(2,1)S(1)}, bf16[64,1152]{1,0:T(8,128)(2,1)S(1)}, u32[]{:S(2)}, u32[]{:S(2)}) collective-permute-start(bf16[64,1152]{1,0:T(8,128)(2,1)S(1)} %slice.101), channel_id=1, source_target_pairs={{0,48},{8,200},{16,0},{24,216},{32,16},{40,232},{48,32},{56,248},{... | collective-permute-start | bytes 442376 | tf_op jit(solution)/shard_map/ppermute | solution.py:43
  31.2 26.0 %copy-start.5 = (bf16[512,1152]{1,0:T(8,128)(2,1)}, bf16[512,1152]{1,0:T(8,128)(2,1)S(1)}, u32[]{:S(2)}) copy-start(bf16[512,1152]{1,0:T(8,128)(2,1)S(1)} %constant_dynamic-update-slice_fusion.p0) | copy-start | bytes 3538948
  31.2 19.0 %collective-permute-start.6 = (bf16[512,1152]{1,0:T(8,128)(2,1)S(1)}, bf16[512,1152]{1,0:T(8,128)(2,1)S(1)}, u32[]{:S(2)}, u32[]{:S(2)}) collective-permute-start(bf16[512,1152]{1,0:T(8,128)(2,1)S(1)} %constant_dynamic-update-slice_fusion.p0), channel_id=1, source_target_pairs={{0,64},{8,24},{16,80},{24,40},{32,96},{40,56},{48,112},{56,8},{64,... | collective-permute-start | bytes 3538952 | tf_op jit(solution)/shard_map/ppermute | solution.py:43
  31.5 19.7 %collective-permute-start.7 = (bf16[512,1152]{1,0:T(8,128)(2,1)S(1)}, bf16[512,1152]{1,0:T(8,128)(2,1)S(1)}, u32[]{:S(2)}, u32[]{:S(2)}) collective-permute-start(bf16[512,1152]{1,0:T(8,128)(2,1)S(1)} %constant_dynamic-update-slice_fusion.p0), channel_id=1, source_target_pairs={{0,192},{8,56},{16,208},{24,8},{32,224},{40,24},{48,240},{56,40},{... | collective-permute-start | bytes 3538952 | tf_op jit(solution)/shard_map/ppermute | solution.py:43
  51.2 23.0 %collective-permute-start.8 = (bf16[256,1152]{1,0:T(8,128)(2,1)}, bf16[256,1152]{1,0:T(8,128)(2,1)}, u32[]{:S(2)}, u32[]{:S(2)}) collective-permute-start(bf16[256,1152]{1,0:T(8,128)(2,1)} %slice.102), channel_id=1, source_target_pairs={{0,64},{8,24},{16,80},{24,40},{32,96},{40,56},{48,112},{56,8},{64,... | collective-permute-start | bytes 1769480 | tf_op jit(solution)/shard_map/ppermute | solution.py:43
  52.1 22.0 %collective-permute-start.9 = (bf16[256,1152]{1,0:T(8,128)(2,1)}, bf16[256,1152]{1,0:T(8,128)(2,1)}, u32[]{:S(2)}, u32[]{:S(2)}) collective-permute-start(bf16[256,1152]{1,0:T(8,128)(2,1)} %slice.103), channel_id=1, source_target_pairs={{0,192},{8,56},{16,208},{24,8},{32,224},{40,24},{48,240},{56,40},{... | collective-permute-start | bytes 1769480 | tf_op jit(solution)/shard_map/ppermute | solution.py:43
  77.9 14.9 %collective-permute-start.15 = (bf16[6,128,128]{2,1,0:T(8,128)(2,1)}, bf16[6,128,128]{2,1,0:T(8,128)(2,1)S(1)}, u32[]{:S(2)}, u32[]{:S(2)}) collective-permute-start(bf16[6,128,128]{2,1,0:T(8,128)(2,1)} %bitcast.12), channel_id=1, source_target_pairs={{0,64},{64,128},{128,192},{192,0},{1,65},{65,129},{129,193},{193,1... | collective-permute-start | bytes 589832 | tf_op jit(solution)/shard_map/ppermute | solution.py:32
  77.9 14.9 %collective-permute-start.16 = (bf16[6,128,128]{2,1,0:T(8,128)(2,1)}, bf16[6,128,128]{2,1,0:T(8,128)(2,1)S(1)}, u32[]{:S(2)}, u32[]{:S(2)}) collective-permute-start(bf16[6,128,128]{2,1,0:T(8,128)(2,1)} %bitcast.13), channel_id=1, source_target_pairs={{0,192},{64,0},{128,64},{192,128},{1,193},{65,1},{129,65},{193,129... | collective-permute-start | bytes 589832 | tf_op jit(solution)/shard_map/ppermute | solution.py:32
  80.6 12.2 %collective-permute-start.17 = (bf16[6,128,128]{2,1,0:T(8,128)(2,1)}, bf16[6,128,128]{2,1,0:T(8,128)(2,1)S(1)}, u32[]{:S(2)}, u32[]{:S(2)}) collective-permute-start(bf16[6,128,128]{2,1,0:T(8,128)(2,1)} %bitcast.14), channel_id=1, source_target_pairs={{0,128},{64,192},{128,0},{192,64},{1,129},{65,193},{129,1},{193,65... | collective-permute-start | bytes 589832 | tf_op jit(solution)/shard_map/ppermute | solution.py:32
  82.6 19.6 %collective-permute-start.11 = (bf16[768,128]{1,0:T(8,128)(2,1)}, bf16[768,128]{1,0:T(8,128)(2,1)S(1)}, u32[]{:S(2)}, u32[]{:S(2)}) collective-permute-start(bf16[768,128]{1,0:T(8,128)(2,1)} %project_columns.1), channel_id=1, source_target_pairs={{0,16},{8,24},{16,32},{24,40},{32,48},{40,56},{48,64},{56,72},{64,... | collective-permute-start | bytes 589832 | tf_op jit(solution)/shard_map/ppermute | solution.py:219
  86.2 16.0 %collective-permute-start.10 = (bf16[256,128]{1,0:T(8,128)(2,1)S(1)}, bf16[256,128]{1,0:T(8,128)(2,1)S(1)}, u32[]{:S(2)}, u32[]{:S(2)}) collective-permute-start(bf16[256,128]{1,0:T(8,128)(2,1)S(1)} %slice.104), channel_id=1, source_target_pairs={{0,32},{8,40},{16,48},{24,56},{32,64},{40,72},{48,80},{56,88},{64,... | collective-permute-start | bytes 196616 | tf_op jit(solution)/shard_map/ppermute | solution.py:221
  99.5 7.2 %collective-permute-start.18 = (bf16[6,128,128]{2,1,0:T(8,128)(2,1)}, bf16[6,128,128]{2,1,0:T(8,128)(2,1)S(1)}, u32[]{:S(2)}, u32[]{:S(2)}) collective-permute-start(bf16[6,128,128]{2,1,0:T(8,128)(2,1)} %get-tuple-element.7), channel_id=1, source_target_pairs={{0,16},{16,32},{32,48},{48,0},{1,17},{17,33},{33,49},{49,1},{2,18}... | collective-permute-start | bytes 589832 | tf_op jit(solution)/shard_map/ppermute | solution.py:32
  99.6 7.7 %collective-permute-start.19 = (bf16[6,128,128]{2,1,0:T(8,128)(2,1)}, bf16[6,128,128]{2,1,0:T(8,128)(2,1)S(1)}, u32[]{:S(2)}, u32[]{:S(2)}) collective-permute-start(bf16[6,128,128]{2,1,0:T(8,128)(2,1)} %get-tuple-element.8), channel_id=1, source_target_pairs={{0,48},{16,0},{32,16},{48,32},{1,49},{17,1},{33,17},{49,33},{2,50}... | collective-permute-start | bytes 589832 | tf_op jit(solution)/shard_map/ppermute | solution.py:32
  102.2 8.0 %collective-permute-start.20 = (bf16[6,128,128]{2,1,0:T(8,128)(2,1)}, bf16[6,128,128]{2,1,0:T(8,128)(2,1)S(1)}, u32[]{:S(2)}, u32[]{:S(2)}) collective-permute-start(bf16[6,128,128]{2,1,0:T(8,128)(2,1)} %get-tuple-element.9), channel_id=1, source_target_pairs={{0,32},{16,48},{32,0},{48,16},{1,33},{17,49},{33,1},{49,17},{2,34}... | collective-permute-start | bytes 589832 | tf_op jit(solution)/shard_map/ppermute | solution.py:32
  102.3 12.8 %collective-permute-start.12 = (bf16[1792,128]{1,0:T(8,128)(2,1)S(1)}, bf16[1792,128]{1,0:T(8,128)(2,1)S(1)}, u32[]{:S(2)}, u32[]{:S(2)}) collective-permute-start(bf16[1792,128]{1,0:T(8,128)(2,1)S(1)} %pad_maximum_fusion.3), channel_id=1, source_target_pairs={{0,8},{8,0},{1,9},{9,1},{2,10},{10,2},{3,11},{11,3},{4,12},{12,4},... | collective-permute-start | bytes 1376264 | tf_op jit(solution)/shard_map/ppermute | solution.py:27
  111.3 35.3 %collective-permute-start.21 = (bf16[3,128,128]{2,1,0:T(8,128)(2,1)S(1)}, bf16[3,128,128]{2,1,0:T(8,128)(2,1)S(1)}, u32[]{:S(2)}, u32[]{:S(2)}) collective-permute-start(bf16[3,128,128]{2,1,0:T(8,128)(2,1)S(1)} %broadcast_select_fusion.16), channel_id=1, source_target_pairs={{0,8},{8,0},{1,9},{9,1},{2,10},{10,2},{3,11},{11,3},{4,12},{12,4},... | collective-permute-start | bytes 294920 | tf_op jit(solution)/shard_map/ppermute | solution.py:27
  131.1 16.2 %collective-permute-start.13 = (bf16[384,512]{1,0:T(8,128)(2,1)S(1)}, bf16[384,512]{1,0:T(8,128)(2,1)S(1)}, u32[]{:S(2)}, u32[]{:S(2)}) collective-permute-start(bf16[384,512]{1,0:T(8,128)(2,1)S(1)} %get-tuple-element.38), channel_id=1, source_target_pairs={{0,8},{8,0},{1,9},{9,1},{2,10},{10,2},{3,11},{11,3},{4,12},{12,4},... | collective-permute-start | bytes 1179656 | tf_op jit(solution)/shard_map/ppermute | solution.py:27
  146.0 1.9 %collective-permute-start.14 = (bf16[384,512]{1,0:T(8,128)(2,1)S(1)}, bf16[384,512]{1,0:T(8,128)(2,1)S(1)}, u32[]{:S(2)}, u32[]{:S(2)}) collective-permute-start(bf16[384,512]{1,0:T(8,128)(2,1)S(1)} %get-tuple-element.40), channel_id=1, source_target_pairs={{0,8},{8,0},{1,9},{9,1},{2,10},{10,2},{3,11},{11,3},{4,12},{12,4},... | collective-permute-start | bytes 1179656 | tf_op jit(solution)/shard_map/ppermute | solution.py:27
  (13 other events, 93.5 us)
Sparse Core Ops, SparseCore 0:
  10.6 69.6 all-gather.1

commit v2 on v1

v2 whole, which is shorter than its diff:
```python
import jax
import jax.numpy as jnp
from jax import lax
from jax.experimental import pallas as pl
from jax.experimental.pallas import tpu as pltpu
from jax.sharding import Mesh, PartitionSpec as P

WINDOW = 1024
BLK = 128
HD = 128
NY = 4
NX = 4
SEQ = ("y", "x", "core")
EPSILON = 1e-06
LOG2E = 1.4426950408889634
MASKED = -1e30
REL = (0, -1, 1, 2)


def normalize(hidden_in, norm_gain):
    wide = hidden_in.astype(jnp.float32)
    mean_square = jnp.mean(wide * wide, axis=1, keepdims=True)
    return (wide * lax.rsqrt(mean_square + EPSILON) * norm_gain.astype(jnp.float32)).astype(jnp.bfloat16)


def other_core(array):
    return lax.ppermute(array, "core", [(0, 1), (1, 0)])


def turn(array, axis, by):
    n = lax.axis_size(axis)
    return lax.ppermute(array, axis, [(i, (i + by) % n) for i in range(n)])


def hop(array, phase, by):
    pairs = []
    for y in range(NY):
        for x in range(NX):
            for core in range(2):
                along_x = (core == 0) == (phase == 1)
                ty, tx = (y, (x + by) % NX) if along_x else ((y + by) % NY, x)
                pairs.append(((y * NX + x) * 2 + core, (ty * NX + tx) * 2 + core))
    return lax.ppermute(array, SEQ, pairs)


def ring_pieces(array, phase):
    half = array.shape[0] // 2
    before = hop(array, phase, 1)
    after = hop(array, phase, -1)
    far_lo = hop(before[:half], phase, 1)
    far_hi = hop(after[half:], phase, -1)
    return [array, before, after, far_lo, far_hi]


def place(difference):
    d = lax.rem(difference, 4)
    return jnp.where(d == 0, 0, jnp.where(d == 3, 1, jnp.where(d == 1, 2, 3)))


def block_order(meta_ref):
    y, x, core = meta_ref[0], meta_ref[1], meta_ref[2]
    places = []
    for outer in REL:
        for inner in REL:
            dy = jnp.where(core == 0, outer, inner)
            dx = jnp.where(core == 0, inner, outer)
            places.append(lax.rem(y + dy + NY, NY) * NX + lax.rem(x + dx + NX, NX))
    return places


def assemble(piece_refs, places, weight_ref, shift=0):
    j = 0
    for piece_ref in piece_refs:
        for start in range(0, piece_ref.shape[0], BLK):
            to = lax.rem(places[j] + shift, NY * NX) * BLK
            weight_ref[pl.ds(pl.multiple_of(to, BLK), BLK), :] = piece_ref[start : start + BLK, :]
            j += 1


def kv_kernel(meta_ref, mine_ref, theirs_ref, p0, p1, p2, p3, p4, ring_ref, made_ref, ring_out_ref, w_ref):
    assemble((p0, p1, p2, p3, p4), block_order(meta_ref), w_ref)
    rows = mine_ref.shape[0]
    core = meta_ref[2]
    for ref, at in ((mine_ref, core * rows), (theirs_ref, (1 - core) * rows)):
        made_ref[pl.ds(pl.multiple_of(at, BLK), rows), :] = jnp.dot(
            ref[...], w_ref[...], preferred_element_type=jnp.float32
        ).astype(jnp.bfloat16)


def project_kv(meta, mine, theirs, pieces, index, ring):
    rows, depth = mine.shape
    anywhere = pl.BlockSpec(memory_space=pl.ANY)
    return pl.pallas_call(
        kv_kernel,
        out_shape=[
            jax.ShapeDtypeStruct((2 * rows, HD), jnp.bfloat16),
            jax.ShapeDtypeStruct(ring.shape, ring.dtype),
        ],
        grid_spec=pltpu.PrefetchScalarGridSpec(
            num_scalar_prefetch=1,
            grid=(1,),
            in_specs=[pl.BlockSpec(mine.shape, lambda i, m: (0, 0))] * 2
            + [pl.BlockSpec((p.shape[0], HD), lambda i, m: (0, index)) for p in pieces]
            + [anywhere],
            out_specs=[pl.BlockSpec((2 * rows, HD), lambda i, m: (0, 0)), anywhere],
            scratch_shapes=[pltpu.VMEM((depth, HD), jnp.bfloat16)],
        ),
        input_output_aliases={8: 1},
        name="project_kv",
    )(meta, mine, theirs, *pieces, ring)


def query_kernel(meta_ref, mine_ref, theirs_ref, p0, p1, p2, p3, p4, made_ref, out_ref, made_out_ref, w_ref):
    assemble((p0, p1, p2, p3, p4), block_order(meta_ref), w_ref)
    rows = mine_ref.shape[0]
    factor = LOG2E / HD**0.5
    for ref, at in ((mine_ref, 0), (theirs_ref, rows)):
        out_ref[at : at + rows, :] = (
            jnp.dot(ref[...], w_ref[...], preferred_element_type=jnp.float32) * factor
        ).astype(jnp.bfloat16)


def project_query(meta, mine, theirs, pieces, width, made):
    rows, depth = mine.shape
    group = 4 * HD
    anywhere = pl.BlockSpec(memory_space=pl.ANY)
    return pl.pallas_call(
        query_kernel,
        out_shape=[
            jax.ShapeDtypeStruct((2 * rows, width), jnp.bfloat16),
            jax.ShapeDtypeStruct(made.shape, made.dtype),
        ],
        grid_spec=pltpu.PrefetchScalarGridSpec(
            num_scalar_prefetch=1,
            grid=(width // group,),
            in_specs=[pl.BlockSpec(mine.shape, lambda i, m: (0, 0))] * 2
            + [pl.BlockSpec((p.shape[0], group), lambda i, m: (0, i)) for p in pieces]
            + [anywhere],
            out_specs=[pl.BlockSpec((2 * rows, group), lambda i, m: (0, i)), anywhere],
            scratch_shapes=[pltpu.VMEM((depth, group), jnp.bfloat16)],
        ),
        input_output_aliases={8: 1},
        name="project_query",
    )(meta, mine, theirs, *pieces, made)


def attend_kernel(meta_ref, q_ref, s2, s1, s0, c2, c1, c0, segq_ref, segk_ref, out_ref, key_ref, v_ref):
    rows, width = out_ref.shape
    span = WINDOW + BLK
    core = meta_ref[2]
    blocks = rows // BLK

    def fill(key_refs, value_refs):
        start = 0
        for key, value in zip(key_refs, value_refs):
            count = key.shape[0]
            key_ref[start : start + count, :] = key[...]
            v_ref[start : start + count, :HD] = value[...]
            start += count

    @pl.when(core == 0)
    def _():
        fill((s2, s1, s0), (c2, c1, c0))

    @pl.when(core != 0)
    def _():
        fill((c2, c1, c0), (s2, s1, s0))

    v_ref[:, HD:] = jnp.ones((v_ref.shape[0], HD), jnp.bfloat16)

    def block(b, carry):
        at = lax.rem(b + core * (blocks // 2), blocks)
        first = pl.multiple_of(at * BLK, BLK)
        mine = pl.multiple_of(b * BLK, BLK)
        row = lax.broadcasted_iota(jnp.int32, (BLK, span), 0)
        col = lax.broadcasted_iota(jnp.int32, (BLK, span), 1)
        near = (col > row) & (col <= row + WINDOW) & (segq_ref[at] == segk_ref[at])
        bias = jnp.where(near, 0.0, MASKED)
        keys = key_ref[pl.ds(first, span), :]
        values = v_ref[pl.ds(first, span), :]
        for head in range(width // HD):
            query = q_ref[pl.ds(mine, BLK), head * HD : (head + 1) * HD]
            scores = lax.dot_general(
                query, keys, (((1,), (1,)), ((), ())), preferred_element_type=jnp.float32
            )
            scores = scores + bias
            top = jnp.max(scores, axis=1, keepdims=True)
            weights = jnp.exp2(scores - top).astype(jnp.bfloat16)
            mixed = jnp.dot(weights, values, preferred_element_type=jnp.float32)
            out_ref[pl.ds(mine, BLK), head * HD : (head + 1) * HD] = (
                mixed[:, :HD] / mixed[:, HD:]
            ).astype(jnp.bfloat16)
        return carry

    lax.fori_loop(0, blocks, block, 0)


def attend(meta, query, width, index, same, cross, segq, segk):
    rows = query.shape[0]
    whole = lambda a: pl.BlockSpec(a.shape, lambda i, m: (0,) * a.ndim)
    rest = (*same, *cross, segq, segk)
    return pl.pallas_call(
        attend_kernel,
        out_shape=jax.ShapeDtypeStruct((rows, width), jnp.bfloat16),
        grid_spec=pltpu.PrefetchScalarGridSpec(
            num_scalar_prefetch=1,
            grid=(1,),
            in_specs=[pl.BlockSpec((rows, width), lambda i, m: (0, index))] + [whole(a) for a in rest],
            out_specs=pl.BlockSpec((rows, width), lambda i, m: (0, 0)),
            scratch_shapes=[
                pltpu.VMEM((WINDOW + rows, HD), jnp.bfloat16),
                pltpu.VMEM((WINDOW + rows, 2 * HD), jnp.bfloat16),
            ],
        ),
        name="attend",
    )(meta, query, *rest)


def out_kernel(
    meta_ref, k0, k1, g0, g1, p0, p1, p2, p3, p4, mine_ref, theirs_ref, mine_out, theirs_out, x_ref, w_ref
):
    rows = mine_ref.shape[0]
    group = k0.shape[1]

    @pl.when(pl.program_id(0) == 0)
    def _():
        for n, ref in enumerate((k0, k1)):
            x_ref[:, n * group : (n + 1) * group] = ref[...]
        for n, ref in enumerate((g0, g1)):
            columns = slice((n + 2) * group, (n + 3) * group)
            x_ref[:rows, columns] = ref[rows:, :]
            x_ref[rows:, columns] = ref[:rows, :]

    assemble((p0, p1, p2, p3, p4), block_order(meta_ref), w_ref, meta_ref[2] * (NY * NX // 2))
    for hidden, out, at in ((mine_ref, mine_out, 0), (theirs_ref, theirs_out, rows)):
        product = jnp.dot(x_ref[at : at + rows, :], w_ref[...], preferred_element_type=jnp.float32)
        out[...] = (hidden[...].astype(jnp.float32) + product).astype(jnp.bfloat16)


def project_out(meta, kept, got, pieces, mine, theirs):
    rows, width = mine.shape
    half = width // 2
    step = 256
    whole = lambda a: pl.BlockSpec(a.shape, lambda i, m: (0, 0))
    hidden = pl.BlockSpec((rows, step), lambda i, m: (0, m[2] * (half // step) + i))
    out = pl.BlockSpec((rows, step), lambda i, m: (0, i))
    return pl.pallas_call(
        out_kernel,
        out_shape=[jax.ShapeDtypeStruct((rows, half), jnp.bfloat16)] * 2,
        grid_spec=pltpu.PrefetchScalarGridSpec(
            num_scalar_prefetch=1,
            grid=(half // step,),
            in_specs=[whole(a) for a in (*kept, *got)]
            + [pl.BlockSpec((p.shape[0], step), lambda i, m: (0, i)) for p in pieces]
            + [hidden, hidden],
            out_specs=[out, out],
            scratch_shapes=[
                pltpu.VMEM((2 * rows, width), jnp.bfloat16),
                pltpu.VMEM((width, step), jnp.bfloat16),
            ],
        ),
        name="project_out",
    )(meta, *kept, *got, *pieces, mine, theirs)


def pick_kernel(meta_ref, source_ref, a, b, c, d, after_ref, oa, ob, oc, od):
    oa[...] = a[...]
    ob[...] = b[...]
    oc[...] = c[...]
    od[...] = d[...]


def pick_blocks(meta, source_of, column, per_chip, after):
    shape = (1,) + column.shape[1:]
    row = NX * per_chip

    def spec(target):
        def index(i, m, source_ref):
            y, x = m[0], m[1]
            source = source_ref[y * row + lax.rem(x + target + NX, NX) * per_chip + i]
            return (place(source // row - y + NY) * per_chip + lax.rem(source, per_chip), 0, 0)

        return pl.BlockSpec(shape, index)

    out = pl.BlockSpec(shape, lambda i, m, source_ref: (i, 0, 0))
    return pl.pallas_call(
        pick_kernel,
        out_shape=[jax.ShapeDtypeStruct((per_chip,) + column.shape[1:], column.dtype)] * 4,
        grid_spec=pltpu.PrefetchScalarGridSpec(
            num_scalar_prefetch=2,
            grid=(per_chip,),
            in_specs=[spec(t) for t in (0, 1, -1, 2)] + [pl.BlockSpec(memory_space=pl.ANY)],
            out_specs=[out] * 4,
        ),
        name="pick_blocks",
    )(meta, source_of, column, column, column, column, after)


def own_kernel(meta_ref, source_ref, a, b, c, d, keep_ref, send_ref):
    per_chip = a.shape[0]
    y, x, core = meta_ref[0], meta_ref[1], meta_ref[2]
    refs = (a, b, c, d)
    half = per_chip // 2
    for i in range(half):
        for out_ref, part in ((keep_ref, core), (send_ref, 1 - core)):
            at = part * half + i
            source = source_ref[(y * NX + x) * per_chip + at]
            where = place(lax.rem(source // per_chip, NX) - x + NX)
            for k in range(4):

                @pl.when(where == k)
                def _(out_ref=out_ref, i=i, at=at, k=k):
                    out_ref[i] = refs[k][at]


def own_blocks(meta, source_of, arrived):
    per_chip = arrived[0].shape[0]
    shape = (per_chip // 2,) + arrived[0].shape[1:]
    whole = lambda s: pl.BlockSpec(s, lambda i, m, source_ref: (0, 0, 0))
    return pl.pallas_call(
        own_kernel,
        out_shape=[jax.ShapeDtypeStruct(shape, jnp.bfloat16)] * 2,
        grid_spec=pltpu.PrefetchScalarGridSpec(
            num_scalar_prefetch=2,
            grid=(1,),
            in_specs=[whole(a.shape) for a in arrived],
            out_specs=[whole(shape)] * 2,
        ),
        name="own_blocks",
    )(meta, source_of, *arrived)


def halves(part0, part1, first_core):
    keep = jnp.where(first_core, part0, part1)
    taken = other_core(jnp.where(first_core, part1, part0))
    return jnp.concatenate(
        [jnp.where(first_core, keep, taken), jnp.where(first_core, taken, keep)], axis=0
    )


def send_on(array, chips, cross):
    count = NY * NX
    pairs = [
        (chip * 2 + core, (chip + chips) * 2 + (1 - core if cross else core))
        for chip in range(count - chips)
        for core in range(2)
    ]
    return lax.ppermute(array, SEQ, pairs)


def shards(hidden_in, norm_gain, w_query, w_key, w_value, w_out, seg_ids, cache_slot):
    row_count, width = hidden_in.shape
    half = width // 2
    y, x, core = (lax.axis_index(a) for a in SEQ)
    first_core = core == 0
    chip = y * NX + x
    meta = jnp.stack([y, x, core]).astype(jnp.int32)

    own = halves(
        jnp.concatenate([w_query[:, :half], w_key], axis=1),
        jnp.concatenate([w_query[:, half:], w_value], axis=1),
        first_core,
    )
    own_out = halves(w_out[:, :half], w_out[:, half:], first_core)
    hidden_theirs = other_core(hidden_in)
    ring = jnp.concatenate(ring_pieces(own, 1), axis=0)
    ring_out = jnp.concatenate(ring_pieces(own_out, 1), axis=0)
    pieces = ring_pieces(ring, 2)

    mine = normalize(hidden_in, norm_gain)
    theirs = normalize(hidden_theirs, norm_gain)
    chip_rows = 2 * row_count

    made, ring_out = project_kv(meta, mine, theirs, pieces, half // HD, ring_out)
    short = WINDOW - chip_rows
    tail = made[chip_rows - short :]
    same = (send_on(tail, 2, False), send_on(made, 1, False), made)
    cross = (send_on(tail, 2, True), send_on(made, 1, True), send_on(made, 0, True))
    pieces_out = ring_pieces(ring_out, 2)
    query, made = project_query(meta, mine, theirs, pieces, half, made)

    seg_pad = jnp.concatenate([jnp.full((WINDOW,), -1, jnp.int32), seg_ids])
    seg_here = lax.dynamic_slice_in_dim(seg_pad, chip * chip_rows, WINDOW + chip_rows, 0)
    blocks = chip_rows // BLK
    segq = seg_here[WINDOW:].reshape(blocks, BLK, 1)
    segk = jnp.stack([seg_here[b * BLK : b * BLK + WINDOW + BLK] for b in range(blocks)])[:, None, :]

    group = 4 * HD
    kept = [attend(meta, query, group, i, same, cross, segq, segk) for i in range(half // group)]
    got = [other_core(a) for a in kept]
    out_mine, out_theirs = project_out(meta, kept, got, pieces_out, hidden_in, hidden_theirs)
    out_got = other_core(out_theirs)
    hidden_out = jnp.concatenate(
        [jnp.where(first_core, out_mine, out_got), jnp.where(first_core, out_got, out_mine)], axis=1
    )

    made = made.reshape(blocks, BLK, HD)
    column = jnp.concatenate([made, turn(made, "y", 1), turn(made, "y", -1), turn(made, "y", 2)], axis=0)
    total = cache_slot.shape[0]
    ids = jnp.arange(total, dtype=jnp.int32)
    source_of = jnp.sum(jnp.where(cache_slot[None, :] == ids[:, None], ids[None, :], 0), axis=1)
    here, right, left, across = pick_blocks(meta, source_of, column, blocks, kept[0])
    arrived = (here, turn(right, "x", 1), turn(left, "x", -1), turn(across, "x", 2))
    cache_keep, cache_send = own_blocks(meta, source_of, arrived)
    cache_got = other_core(cache_send)
    kv_cache = jnp.concatenate(
        [jnp.where(first_core, cache_keep, cache_got), jnp.where(first_core, cache_got, cache_keep)], axis=2
    ).reshape(row_count, 2 * HD)
    return (hidden_out, kv_cache)


def solution(mesh):
    grid = Mesh(mesh.devices.reshape(NY, NX, 2, mesh.devices.shape[1]), SEQ + ("grp",))
    everywhere = P(("grp",) + SEQ, None)
    in_specs = (
        everywhere,
        P(),
        P(SEQ, None),
        P(SEQ, None),
        P(SEQ, None),
        P(SEQ, None),
        P("grp"),
        P("grp"),
    )
    return jax.shard_map(
        shards, mesh=grid, in_specs=in_specs, out_specs=(everywhere, everywhere), check_vma=False
    )
```

time: 165 us -> 175 us (1.061)
  starting transfers between devices: 38.1 us -> 60.9 us
  waiting for transfers between devices: 17.2 us -> 31.2 us
  between operations: 14.4 us -> 1.13 us
  other arithmetic: 24.8 us -> 14.2 us
  matrix products: 7.87 us -> 0 us
  Pallas kernels: 46.6 us -> 52.6 us
    ppermute x8 -> x16, starting transfers between devices: 11 us -> 27.5 us  [hop(): return lax.ppermute(array, SEQ, pairs)]
    pallas_call x3 -> x5, Pallas kernels: 19.3 us -> 29.7 us  [the longest x1 9.36 us: project_out(): pl.pallas_call(out_kernel, out_shape=[jax.ShapeDtypeStruct((rows, half),...]
    select_n x11 -> x3, other arithmetic: 10.8 us -> 1.91 us  [the longest x2 1.8 us: halves(): taken = other_core(jnp.where(first_core, part1, part0))]
    ppermute x8 -> x16, waiting for transfers between devices: 12.4 us -> 20.5 us  [hop(): return lax.ppermute(array, SEQ, pairs)]
    unnamed x32 -> x61, local copies, waits for them, and re-layouts: 1.17 us -> 9.1 us
    dot_general x1 -> x0, matrix products: 7.87 us -> none  [shards(): jnp.dot(columns, w_out_whole, preferred_element_type=jnp.float32)]
    ppermute x2 -> x5, starting transfers between devices: 8.31 us -> 14.3 us  [send_on(): return lax.ppermute(array, SEQ, pairs)]
    ppermute x6, waiting for transfers between devices: 3.51 us -> 9.47 us  [turn(): return lax.ppermute(array, axis, [(i, (i + by) % n) for i in range(n)])]
  transfers between devices with their start and end apart: 23 -> 34, of which waited for: 7 -> 11; matrix products, arithmetic and copies ran while one was open for 24% -> 12% of each run, Pallas kernels for 28% -> 28%
where the time goes in v2:
time: 175 us; the launch traced here: 174 us
  starting transfers between devices  60.9 us (35%)
  Pallas kernels  52.6 us (30%)
  waiting for transfers between devices  31.2 us (18%)
  other arithmetic  14.2 us (8%)
  local copies, waits for them, and re-layouts  13.7 us (8%)
    ppermute x16, starting transfers between devices, hop(): return lax.ppermute(array, SEQ, pairs)  27.5 us
    pallas_call x2, Pallas kernels, attend(): pl.pallas_call(attend_kernel, out_shape=jax.ShapeDtypeStruct((rows, width...  22.9 us
    ppermute x16, waiting for transfers between devices, hop(): return lax.ppermute(array, SEQ, pairs)  20.5 us
    ppermute x5, starting transfers between devices, send_on(): return lax.ppermute(array, SEQ, pairs)  14.3 us
    ppermute x6, starting transfers between devices, turn(): return lax.ppermute(array, axis, [(i, (i + by) % n) for i in range(n)])  10.3 us
    ppermute x6, waiting for transfers between devices, turn(): return lax.ppermute(array, axis, [(i, (i + by) % n) for i in range(n)])  9.47 us
    pallas_call x1, Pallas kernels, project_out(): pl.pallas_call(out_kernel, out_shape=[jax.ShapeDtypeStruct((rows, half),...  9.36 us
    unnamed x61, local copies, waits for them, and re-layouts  9.1 us
  transfers between devices with their start and end apart: 34, of which 11 were waited for; matrix products, arithmetic and copies ran while one was open for 12% of the time, Pallas kernels for 28%

profile of v2, /device:TPU:1, one launch (start us, length us, event | category | flops | bytes accessed | tf_op | source)
XLA Modules:
  0.0 173.7 jit_solution(11713761411100614051)
XLA Ops:
  1.7 3.3 %collective-permute-start.10 = (bf16[64,1024]{1,0:T(8,128)(2,1)S(1)}, bf16[64,1024]{1,0:T(8,128)(2,1)S(1)}, u32[]{:S(2)}, u32[]{:S(2)}) collective-permute-start(bf16[64,1024]{1,0:T(8,128)(2,1)S(1)} %broadcast_select_fusion.8), channel_id=1, source_target_pairs={{0,8},{8,0},{1,9},{9,1},{2,10},{10,2},{3,11},{11,3},{4,12},{12,4},... | collective-permute-start | bytes 393224 | tf_op jit(solution)/shard_map/ppermute | solution.py:27
  10.2 2.7 %collective-permute-start.3 = (bf16[128,1152]{1,0:T(8,128)(2,1)S(1)}, bf16[128,1152]{1,0:T(8,128)(2,1)S(1)}, u32[]{:S(2)}, u32[]{:S(2)}) collective-permute-start(bf16[128,1152]{1,0:T(8,128)(2,1)S(1)} %pad_maximum_fusion.2), channel_id=1, source_target_pairs={{0,48},{8,200},{16,0},{24,216},{32,16},{40,232},{48,32},{56,248},{... | collective-permute-start | bytes 884744 | tf_op jit(solution)/shard_map/ppermute | solution.py:43
  17.4 2.7 %collective-permute-start.5 = (bf16[64,1152]{1,0:T(8,128)(2,1)S(1)}, bf16[64,1152]{1,0:T(8,128)(2,1)S(1)}, u32[]{:S(2)}, u32[]{:S(2)}) collective-permute-start(bf16[64,1152]{1,0:T(8,128)(2,1)S(1)} %slice.92), channel_id=1, source_target_pairs={{0,48},{8,200},{16,0},{24,216},{32,16},{40,232},{48,32},{56,248},{... | collective-permute-start | bytes 442376 | tf_op jit(solution)/shard_map/ppermute | solution.py:43
  26.5 2.7 %collective-permute-start.14 = (bf16[64,1024]{1,0:T(8,128)(2,1)S(1)}, bf16[64,1024]{1,0:T(8,128)(2,1)S(1)}, u32[]{:S(2)}, u32[]{:S(2)}) collective-permute-start(bf16[64,1024]{1,0:T(8,128)(2,1)S(1)} %slice.96), channel_id=1, source_target_pairs={{0,48},{8,200},{16,0},{24,216},{32,16},{40,232},{48,32},{56,248},{... | collective-permute-start | bytes 393224 | tf_op jit(solution)/shard_map/ppermute | solution.py:43
  34.9 6.0 %collective-permute-done.6.p1 = bf16[512,1152]{1,0:T(8,128)(2,1)S(1)} collective-permute-done((bf16[512,1152]{1,0:T(8,128)(2,1)S(1)}, bf16[512,1152]{1,0:T(8,128)(2,1)S(1)}, u32[]{:S(2)}, u32[]{:S(2)}) %collective-permute-start.6) | collective-permute-done | bytes 1179680 | tf_op jit(solution)/shard_map/ppermute | solution.py:43
  43.3 2.9 %collective-permute-start.9 = (bf16[256,1152]{1,0:T(8,128)(2,1)S(1)}, bf16[256,1152]{1,0:T(8,128)(2,1)S(1)}, u32[]{:S(2)}, u32[]{:S(2)}) collective-permute-start(bf16[256,1152]{1,0:T(8,128)(2,1)S(1)} %slice.94), channel_id=1, source_target_pairs={{0,192},{8,56},{16,208},{24,8},{32,224},{40,24},{48,240},{56,40},{... | collective-permute-start | bytes 1769480 | tf_op jit(solution)/shard_map/ppermute | solution.py:43
  48.6 3.7 %collective-permute-done.8.p3 = bf16[256,1152]{1,0:T(8,128)(2,1)S(1)} collective-permute-done((bf16[256,1152]{1,0:T(8,128)(2,1)S(1)}, bf16[256,1152]{1,0:T(8,128)(2,1)S(1)}, u32[]{:S(2)}, u32[]{:S(2)}) %collective-permute-start.8) | collective-permute-done | bytes 589856 | tf_op jit(solution)/shard_map/ppermute | solution.py:43
  53.8 4.5 %project_kv.1 = (bf16[768,128]{1,0:T(8,128)(2,1)}, bf16[512,1024]{1,0:T(8,128)(2,1)}) custom-call(s32[3]{0:T(128)} %pad_add_fusion.meta_ref, bf16[384,2048]{1,0:T(8,128)(2,1)} %get-tuple-element.47.mine_ref, bf16[384,2048]{1,0:T(8,128)(2,1)} %get-tuple-element.46.theirs_ref, bf16[512,1152]{1,0:T(8,128)(2,1)} %copy-done.4, ...), custom_call_target="tpu_custom_call", output_to_operand_aliasing={{1}: (8, {})} | custom-call | tf_op jit(solution)/shard_map/project_kv/pallas_call | solution.py:93
  58.4 3.4 %collective-permute-start.23 = (bf16[512,1024]{1,0:T(8,128)(2,1)}, bf16[512,1024]{1,0:T(8,128)(2,1)S(1)}, u32[]{:S(2)}, u32[]{:S(2)}) collective-permute-start(bf16[512,1024]{1,0:T(8,128)(2,1)} %get-tuple-element.16.p0), channel_id=1, source_target_pairs={{0,192},{8,56},{16,208},{24,8},{32,224},{40,24},{48,240},{56,40},{... | collective-permute-start | bytes 3145736 | tf_op jit(solution)/shard_map/ppermute | solution.py:43
  62.7 3.1 %collective-permute-start.15 = (bf16[256,128]{1,0:T(8,128)(2,1)S(1)}, bf16[256,128]{1,0:T(8,128)(2,1)S(1)}, u32[]{:S(2)}, u32[]{:S(2)}) collective-permute-start(bf16[256,128]{1,0:T(8,128)(2,1)S(1)} %slice.80), channel_id=1, source_target_pairs={{0,32},{8,40},{16,48},{24,56},{32,64},{40,72},{48,80},{56,88},{64,... | collective-permute-start | bytes 196616 | tf_op jit(solution)/shard_map/ppermute | solution.py:348
  65.7 5.7 %collective-permute-start.17 = (bf16[256,128]{1,0:T(8,128)(2,1)S(1)}, bf16[256,128]{1,0:T(8,128)(2,1)S(1)}, u32[]{:S(2)}, u32[]{:S(2)}) collective-permute-start(bf16[256,128]{1,0:T(8,128)(2,1)S(1)} %slice.80), channel_id=1, source_target_pairs={{0,40},{8,32},{16,56},{24,48},{32,72},{40,64},{48,88},{56,80},{64,... | collective-permute-start | bytes 196616 | tf_op jit(solution)/shard_map/ppermute | solution.py:348
  71.5 3.1 %collective-permute-start.16 = (bf16[768,128]{1,0:T(8,128)(2,1)}, bf16[768,128]{1,0:T(8,128)(2,1)S(1)}, u32[]{:S(2)}, u32[]{:S(2)}) collective-permute-start(bf16[768,128]{1,0:T(8,128)(2,1)} %get-tuple-element.14.s0), channel_id=1, source_target_pairs={{0,16},{8,24},{16,32},{24,40},{32,48},{40,56},{48,64},{56,72},{64,... | collective-permute-start | bytes 589832 | tf_op jit(solution)/shard_map/ppermute | solution.py:348
  80.5 8.3 %project_query.1 = (bf16[768,1024]{1,0:T(8,128)(2,1)}, bf16[768,128]{1,0:T(8,128)(2,1)}) custom-call(s32[3]{0:T(128)} %pad_add_fusion.meta_ref, bf16[384,2048]{1,0:T(8,128)(2,1)} %get-tuple-element.47.mine_ref, bf16[384,2048]{1,0:T(8,128)(2,1)} %get-tuple-element.46.theirs_ref, bf16[512,1152]{1,0:T(8,128)(2,1)} %copy-done.4, ...), custom_call_target="tpu_custom_call", output_to_operand_aliasing={{1}: (8, {})} | custom-call | tf_op jit(solution)/shard_map/project_query/pallas_call | solution.py:127
  89.7 11.5 %attend.3.k1 = bf16[768,512]{1,0:T(8,128)(2,1)} custom-call(s32[3]{0:T(128)} %pad_add_fusion.meta_ref, bf16[768,1024]{1,0:T(8,128)(2,1)} %get-tuple-element.15.q_ref, bf16[256,128]{1,0:T(8,128)(2,1)} %copy-done.17, bf16[768,128]{1,0:T(8,128)(2,1)} %copy-done.13, bf16[768,128]{1,0:T(8,128)(2,1)} %get-tuple-element.14.s0, bf16[256,128]{1,0:T(8,128)(2,1)} %copy-done.18, ...), custom_call_target="tpu_custom_call" | custom-call | tf_op jit(solution)/shard_map/attend/pallas_call | solution.py:202
  101.2 11.5 %attend.2.k0.after_ref = bf16[768,512]{1,0:T(8,128)(2,1)} custom-call(s32[3]{0:T(128)} %pad_add_fusion.meta_ref, bf16[768,1024]{1,0:T(8,128)(2,1)} %get-tuple-element.15.q_ref, bf16[256,128]{1,0:T(8,128)(2,1)} %copy-done.17, bf16[768,128]{1,0:T(8,128)(2,1)} %copy-done.13, bf16[768,128]{1,0:T(8,128)(2,1)} %get-tuple-element.14.s0, ...), custom_call_target="tpu_custom_call" | custom-call | tf_op jit(solution)/shard_map/attend/pallas_call | solution.py:202
  113.2 2.7 %collective-permute-start.24 = (bf16[256,1024]{1,0:T(8,128)(2,1)S(1)}, bf16[256,1024]{1,0:T(8,128)(2,1)S(1)}, u32[]{:S(2)}, u32[]{:S(2)}) collective-permute-start(bf16[256,1024]{1,0:T(8,128)(2,1)S(1)} %slice.97), channel_id=1, source_target_pairs={{0,64},{8,24},{16,80},{24,40},{32,96},{40,56},{48,112},{56,8},{64,... | collective-permute-start | bytes 1572872 | tf_op jit(solution)/shard_map/ppermute | solution.py:43
  115.9 4.5 %collective-permute-start.25 = (bf16[256,1024]{1,0:T(8,128)(2,1)S(1)}, bf16[256,1024]{1,0:T(8,128)(2,1)}, u32[]{:S(2)}, u32[]{:S(2)}) collective-permute-start(bf16[256,1024]{1,0:T(8,128)(2,1)S(1)} %slice.98), channel_id=1, source_target_pairs={{0,192},{8,56},{16,208},{24,8},{32,224},{40,24},{48,240},{56,40},{... | collective-permute-start | bytes 1572872 | tf_op jit(solution)/shard_map/ppermute | solution.py:43
  123.2 4.0 %collective-permute-done.24.p3 = bf16[256,1024]{1,0:T(8,128)(2,1)S(1)} collective-permute-done((bf16[256,1024]{1,0:T(8,128)(2,1)S(1)}, bf16[256,1024]{1,0:T(8,128)(2,1)S(1)}, u32[]{:S(2)}, u32[]{:S(2)}) %collective-permute-start.24) | collective-permute-done | bytes 524320 | tf_op jit(solution)/shard_map/ppermute | solution.py:43
  128.0 9.4 %project_out.1 = (bf16[384,1024]{1,0:T(8,128)(2,1)}, bf16[384,1024]{1,0:T(8,128)(2,1)}) custom-call(s32[3]{0:T(128)} %pad_add_fusion.meta_ref, bf16[768,512]{1,0:T(8,128)(2,1)} %attend.2.k0.after_ref, bf16[768,512]{1,0:T(8,128)(2,1)} %attend.3.k1, bf16[768,512]{1,0:T(8,128)(2,1)} %collective-permute-done.20.g0, bf16[768,512]{1,0:T(8,128)(2,1)} %copy-done.12, ...), custom_call_target="tpu_custom_call" | custom-call | tf_op jit(solution)/shard_map/project_out/pallas_call | solution.py:247
  137.4 3.6 %collective-permute-start.26 = (bf16[384,1024]{1,0:T(8,128)(2,1)}, bf16[384,1024]{1,0:T(8,128)(2,1)S(1)}, u32[]{:S(2)}, u32[]{:S(2)}) collective-permute-start(bf16[384,1024]{1,0:T(8,128)(2,1)} %get-tuple-element.18), channel_id=1, source_target_pairs={{0,8},{8,0},{1,9},{9,1},{2,10},{10,2},{3,11},{11,3},{4,12},{12,4},... | collective-permute-start | bytes 2359304 | tf_op jit(solution)/shard_map/ppermute | solution.py:27
  143.5 4.8 %pick_blocks.1 = (bf16[6,128,128]{2,1,0:T(8,128)(2,1)}, bf16[6,128,128]{2,1,0:T(8,128)(2,1)}, bf16[6,128,128]{2,1,0:T(8,128)(2,1)}, bf16[6,128,128]{2,1,0:T(8,128)(2,1)}) custom-call(s32[3]{0:T(128)} %pad_add_fusion.meta_ref, s32[96]{0:T(128)} %select_reduce_fusion.source_ref, bf16[24,128,128]{2,1,0:T(8,128)(2,1)} %pad_maximum_fusion.1.a.b.c.d, ...), custom_call_target="tpu_custom_call" | custom-call | tf_op jit(solution)/shard_map/pick_blocks/pallas_call | solution.py:286
  149.1 5.8 %collective-permute-start.31 = (bf16[6,128,128]{2,1,0:T(8,128)(2,1)}, bf16[6,128,128]{2,1,0:T(8,128)(2,1)S(1)}, u32[]{:S(2)}, u32[]{:S(2)}) collective-permute-start(bf16[6,128,128]{2,1,0:T(8,128)(2,1)} %get-tuple-element.22), channel_id=1, source_target_pairs={{0,48},{16,0},{32,16},{48,32},{1,49},{17,1},{33,17},{49,33},{2,50}... | collective-permute-start | bytes 589832 | tf_op jit(solution)/shard_map/ppermute | solution.py:32
  156.0 4.3 %collective-permute-done.30.b = bf16[6,128,128]{2,1,0:T(8,128)(2,1)S(1)} collective-permute-done((bf16[6,128,128]{2,1,0:T(8,128)(2,1)}, bf16[6,128,128]{2,1,0:T(8,128)(2,1)S(1)}, u32[]{:S(2)}, u32[]{:S(2)}) %collective-permute-start.30) | collective-permute-done | bytes 196640 | tf_op jit(solution)/shard_map/ppermute | solution.py:32
  160.2 3.5 %collective-permute-done.31.c = bf16[6,128,128]{2,1,0:T(8,128)(2,1)S(1)} collective-permute-done((bf16[6,128,128]{2,1,0:T(8,128)(2,1)}, bf16[6,128,128]{2,1,0:T(8,128)(2,1)S(1)}, u32[]{:S(2)}, u32[]{:S(2)}) %collective-permute-start.31) | collective-permute-done | bytes 196640 | tf_op jit(solution)/shard_map/ppermute | solution.py:32
  (156 shorter events, 54.9 us)
Async XLA Ops:
  6.9 27.6 %collective-permute-start = (bf16[384,2048]{1,0:T(8,128)(2,1)}, bf16[384,2048]{1,0:T(8,128)(2,1)S(1)}, u32[]{:S(2)}, u32[]{:S(2)}) collective-permute-start(bf16[384,2048]{1,0:T(8,128)(2,1)} %mine_ref.1), channel_id=1, source_target_pairs={{0,8},{8,0},{1,9},{9,1},{2,10},{10,2},{3,11},{11,3},{4,12},{12,4},... | collective-permute-start | bytes 4718600 | tf_op jit(solution)/shard_map/ppermute | solution.py:27
  13.6 12.7 %collective-permute-start.11 = (bf16[128,1024]{1,0:T(8,128)(2,1)S(1)}, bf16[128,1024]{1,0:T(8,128)(2,1)S(1)}, u32[]{:S(2)}, u32[]{:S(2)}) collective-permute-start(bf16[128,1024]{1,0:T(8,128)(2,1)S(1)} %pad_maximum_fusion.3), channel_id=1, source_target_pairs={{0,16},{8,72},{16,32},{24,88},{32,48},{40,104},{48,0},{56,120},{64... | collective-permute-start | bytes 786440 | tf_op jit(solution)/shard_map/ppermute | solution.py:43
  13.7 12.8 %collective-permute-start.12 = (bf16[128,1024]{1,0:T(8,128)(2,1)S(1)}, bf16[128,1024]{1,0:T(8,128)(2,1)S(1)}, u32[]{:S(2)}, u32[]{:S(2)}) collective-permute-start(bf16[128,1024]{1,0:T(8,128)(2,1)S(1)} %pad_maximum_fusion.3), channel_id=1, source_target_pairs={{0,48},{8,200},{16,0},{24,216},{32,16},{40,232},{48,32},{56,248},{... | collective-permute-start | bytes 786440 | tf_op jit(solution)/shard_map/ppermute | solution.py:43
  22.9 18.0 %collective-permute-start.6 = (bf16[512,1152]{1,0:T(8,128)(2,1)S(1)}, bf16[512,1152]{1,0:T(8,128)(2,1)S(1)}, u32[]{:S(2)}, u32[]{:S(2)}) collective-permute-start(bf16[512,1152]{1,0:T(8,128)(2,1)S(1)} %constant_dynamic-update-slice_fusion.p0), channel_id=1, source_target_pairs={{0,64},{8,24},{16,80},{24,40},{32,96},{40,56},{48,112},{56,8},{64,... | collective-permute-start | bytes 3538952 | tf_op jit(solution)/shard_map/ppermute | solution.py:43
  23.0 19.1 %collective-permute-start.7 = (bf16[512,1152]{1,0:T(8,128)(2,1)S(1)}, bf16[512,1152]{1,0:T(8,128)(2,1)S(1)}, u32[]{:S(2)}, u32[]{:S(2)}) collective-permute-start(bf16[512,1152]{1,0:T(8,128)(2,1)S(1)} %constant_dynamic-update-slice_fusion.p0), channel_id=1, source_target_pairs={{0,192},{8,56},{16,208},{24,8},{32,224},{40,24},{48,240},{56,40},{... | collective-permute-start | bytes 3538952 | tf_op jit(solution)/shard_map/ppermute | solution.py:43
  42.0 10.3 %collective-permute-start.8 = (bf16[256,1152]{1,0:T(8,128)(2,1)S(1)}, bf16[256,1152]{1,0:T(8,128)(2,1)S(1)}, u32[]{:S(2)}, u32[]{:S(2)}) collective-permute-start(bf16[256,1152]{1,0:T(8,128)(2,1)S(1)} %slice.93), channel_id=1, source_target_pairs={{0,64},{8,24},{16,80},{24,40},{32,96},{40,56},{48,112},{56,8},{64,... | collective-permute-start | bytes 1769480 | tf_op jit(solution)/shard_map/ppermute | solution.py:43
  58.4 54.7 %collective-permute-start.22 = (bf16[512,1024]{1,0:T(8,128)(2,1)}, bf16[512,1024]{1,0:T(8,128)(2,1)S(1)}, u32[]{:S(2)}, u32[]{:S(2)}) collective-permute-start(bf16[512,1024]{1,0:T(8,128)(2,1)} %get-tuple-element.16.p0), channel_id=1, source_target_pairs={{0,64},{8,24},{16,80},{24,40},{32,96},{40,56},{48,112},{56,8},{64,... | collective-permute-start | bytes 3145736 | tf_op jit(solution)/shard_map/ppermute | solution.py:43
  58.4 57.5 %collective-permute-start.23 = (bf16[512,1024]{1,0:T(8,128)(2,1)}, bf16[512,1024]{1,0:T(8,128)(2,1)S(1)}, u32[]{:S(2)}, u32[]{:S(2)}) collective-permute-start(bf16[512,1024]{1,0:T(8,128)(2,1)} %get-tuple-element.16.p0), channel_id=1, source_target_pairs={{0,192},{8,56},{16,208},{24,8},{32,224},{40,24},{48,240},{56,40},{... | collective-permute-start | bytes 3145736 | tf_op jit(solution)/shard_map/ppermute | solution.py:43
  62.7 11.9 %collective-permute-start.15 = (bf16[256,128]{1,0:T(8,128)(2,1)S(1)}, bf16[256,128]{1,0:T(8,128)(2,1)S(1)}, u32[]{:S(2)}, u32[]{:S(2)}) collective-permute-start(bf16[256,128]{1,0:T(8,128)(2,1)S(1)} %slice.80), channel_id=1, source_target_pairs={{0,32},{8,40},{16,48},{24,56},{32,64},{40,72},{48,80},{56,88},{64,... | collective-permute-start | bytes 196616 | tf_op jit(solution)/shard_map/ppermute | solution.py:348
  65.7 10.4 %collective-permute-start.17 = (bf16[256,128]{1,0:T(8,128)(2,1)S(1)}, bf16[256,128]{1,0:T(8,128)(2,1)S(1)}, u32[]{:S(2)}, u32[]{:S(2)}) collective-permute-start(bf16[256,128]{1,0:T(8,128)(2,1)S(1)} %slice.80), channel_id=1, source_target_pairs={{0,40},{8,32},{16,56},{24,48},{32,72},{40,64},{48,88},{56,80},{64,... | collective-permute-start | bytes 196616 | tf_op jit(solution)/shard_map/ppermute | solution.py:348
  71.5 17.4 %collective-permute-start.16 = (bf16[768,128]{1,0:T(8,128)(2,1)}, bf16[768,128]{1,0:T(8,128)(2,1)S(1)}, u32[]{:S(2)}, u32[]{:S(2)}) collective-permute-start(bf16[768,128]{1,0:T(8,128)(2,1)} %get-tuple-element.14.s0), channel_id=1, source_target_pairs={{0,16},{8,24},{16,32},{24,40},{32,48},{40,56},{48,64},{56,72},{64,... | collective-permute-start | bytes 589832 | tf_op jit(solution)/shard_map/ppermute | solution.py:348
  74.6 14.3 %collective-permute-start.18 = (bf16[768,128]{1,0:T(8,128)(2,1)}, bf16[768,128]{1,0:T(8,128)(2,1)S(1)}, u32[]{:S(2)}, u32[]{:S(2)}) collective-permute-start(bf16[768,128]{1,0:T(8,128)(2,1)} %get-tuple-element.14.s0), channel_id=1, source_target_pairs={{0,24},{8,16},{16,40},{24,32},{32,56},{40,48},{48,72},{56,64},{64,... | collective-permute-start | bytes 589832 | tf_op jit(solution)/shard_map/ppermute | solution.py:348
  76.2 12.7 %collective-permute-start.19 = (bf16[768,128]{1,0:T(8,128)(2,1)}, bf16[768,128]{1,0:T(8,128)(2,1)S(1)}, u32[]{:S(2)}, u32[]{:S(2)}) collective-permute-start(bf16[768,128]{1,0:T(8,128)(2,1)} %get-tuple-element.14.s0), channel_id=1, source_target_pairs={{0,8},{8,0},{16,24},{24,16},{32,40},{40,32},{48,56},{56,48},{64,72... | collective-permute-start | bytes 589832 | tf_op jit(solution)/shard_map/ppermute | solution.py:348
  101.1 19.8 %collective-permute-start.21 = (bf16[768,512]{1,0:T(8,128)(2,1)}, bf16[768,512]{1,0:T(8,128)(2,1)S(1)}, u32[]{:S(2)}, u32[]{:S(2)}) collective-permute-start(bf16[768,512]{1,0:T(8,128)(2,1)} %attend.3.k1), channel_id=1, source_target_pairs={{0,8},{8,0},{1,9},{9,1},{2,10},{10,2},{3,11},{11,3},{4,12},{12,4},... | collective-permute-start | bytes 2359304 | tf_op jit(solution)/shard_map/ppermute | solution.py:27
  112.6 10.5 %collective-permute-start.20 = (bf16[768,512]{1,0:T(8,128)(2,1)}, bf16[768,512]{1,0:T(8,128)(2,1)}, u32[]{:S(2)}, u32[]{:S(2)}) collective-permute-start(bf16[768,512]{1,0:T(8,128)(2,1)} %attend.2.k0.after_ref), channel_id=1, source_target_pairs={{0,8},{8,0},{1,9},{9,1},{2,10},{10,2},{3,11},{11,3},{4,12},{12,4},... | collective-permute-start | bytes 2359304 | tf_op jit(solution)/shard_map/ppermute | solution.py:27
  113.2 14.0 %collective-permute-start.24 = (bf16[256,1024]{1,0:T(8,128)(2,1)S(1)}, bf16[256,1024]{1,0:T(8,128)(2,1)S(1)}, u32[]{:S(2)}, u32[]{:S(2)}) collective-permute-start(bf16[256,1024]{1,0:T(8,128)(2,1)S(1)} %slice.97), channel_id=1, source_target_pairs={{0,64},{8,24},{16,80},{24,40},{32,96},{40,56},{48,112},{56,8},{64,... | collective-permute-start | bytes 1572872 | tf_op jit(solution)/shard_map/ppermute | solution.py:43
  115.9 12.1 %collective-permute-start.25 = (bf16[256,1024]{1,0:T(8,128)(2,1)S(1)}, bf16[256,1024]{1,0:T(8,128)(2,1)}, u32[]{:S(2)}, u32[]{:S(2)}) collective-permute-start(bf16[256,1024]{1,0:T(8,128)(2,1)S(1)} %slice.98), channel_id=1, source_target_pairs={{0,192},{8,56},{16,208},{24,8},{32,224},{40,24},{48,240},{56,40},{... | collective-permute-start | bytes 1572872 | tf_op jit(solution)/shard_map/ppermute | solution.py:43
  120.5 21.1 %collective-permute-start.27 = (bf16[6,128,128]{2,1,0:T(8,128)(2,1)S(1)}, bf16[6,128,128]{2,1,0:T(8,128)(2,1)S(1)}, u32[]{:S(2)}, u32[]{:S(2)}) collective-permute-start(bf16[6,128,128]{2,1,0:T(8,128)(2,1)S(1)} %bitcast.7), channel_id=1, source_target_pairs={{0,64},{64,128},{128,192},{192,0},{1,65},{65,129},{129,193},{193,1... | collective-permute-start | bytes 589832 | tf_op jit(solution)/shard_map/ppermute | solution.py:32
  121.0 20.6 %collective-permute-start.28 = (bf16[6,128,128]{2,1,0:T(8,128)(2,1)S(1)}, bf16[6,128,128]{2,1,0:T(8,128)(2,1)S(1)}, u32[]{:S(2)}, u32[]{:S(2)}) collective-permute-start(bf16[6,128,128]{2,1,0:T(8,128)(2,1)S(1)} %bitcast.8), channel_id=1, source_target_pairs={{0,192},{64,0},{128,64},{192,128},{1,193},{65,1},{129,65},{193,129... | collective-permute-start | bytes 589832 | tf_op jit(solution)/shard_map/ppermute | solution.py:32
  123.2 18.4 %collective-permute-start.29 = (bf16[6,128,128]{2,1,0:T(8,128)(2,1)S(1)}, bf16[6,128,128]{2,1,0:T(8,128)(2,1)}, u32[]{:S(2)}, u32[]{:S(2)}) collective-permute-start(bf16[6,128,128]{2,1,0:T(8,128)(2,1)S(1)} %bitcast.9), channel_id=1, source_target_pairs={{0,128},{64,192},{128,0},{192,64},{1,129},{65,193},{129,1},{193,65... | collective-permute-start | bytes 589832 | tf_op jit(solution)/shard_map/ppermute | solution.py:32
  137.4 35.0 %collective-permute-start.26 = (bf16[384,1024]{1,0:T(8,128)(2,1)}, bf16[384,1024]{1,0:T(8,128)(2,1)S(1)}, u32[]{:S(2)}, u32[]{:S(2)}) collective-permute-start(bf16[384,1024]{1,0:T(8,128)(2,1)} %get-tuple-element.18), channel_id=1, source_target_pairs={{0,8},{8,0},{1,9},{9,1},{2,10},{10,2},{3,11},{11,3},{4,12},{12,4},... | collective-permute-start | bytes 2359304 | tf_op jit(solution)/shard_map/ppermute | solution.py:27
  148.3 11.9 %collective-permute-start.30 = (bf16[6,128,128]{2,1,0:T(8,128)(2,1)}, bf16[6,128,128]{2,1,0:T(8,128)(2,1)S(1)}, u32[]{:S(2)}, u32[]{:S(2)}) collective-permute-start(bf16[6,128,128]{2,1,0:T(8,128)(2,1)} %get-tuple-element.21), channel_id=1, source_target_pairs={{0,16},{16,32},{32,48},{48,0},{1,17},{17,33},{33,49},{49,1},{2,18}... | collective-permute-start | bytes 589832 | tf_op jit(solution)/shard_map/ppermute | solution.py:32
  149.1 14.6 %collective-permute-start.31 = (bf16[6,128,128]{2,1,0:T(8,128)(2,1)}, bf16[6,128,128]{2,1,0:T(8,128)(2,1)S(1)}, u32[]{:S(2)}, u32[]{:S(2)}) collective-permute-start(bf16[6,128,128]{2,1,0:T(8,128)(2,1)} %get-tuple-element.22), channel_id=1, source_target_pairs={{0,48},{16,0},{32,16},{48,32},{1,49},{17,1},{33,17},{49,33},{2,50}... | collective-permute-start | bytes 589832 | tf_op jit(solution)/shard_map/ppermute | solution.py:32
  154.9 10.6 %collective-permute-start.32 = (bf16[6,128,128]{2,1,0:T(8,128)(2,1)}, bf16[6,128,128]{2,1,0:T(8,128)(2,1)S(1)}, u32[]{:S(2)}, u32[]{:S(2)}) collective-permute-start(bf16[6,128,128]{2,1,0:T(8,128)(2,1)} %get-tuple-element.23), channel_id=1, source_target_pairs={{0,32},{16,48},{32,0},{48,16},{1,33},{17,49},{33,1},{49,17},{2,34}... | collective-permute-start | bytes 589832 | tf_op jit(solution)/shard_map/ppermute | solution.py:32
  (37 other events, 285.6 us)

commit v3 on v2

--- a/solution.py
+++ b/solution.py
@@ -110,7 +110,7 @@
     )(meta, mine, theirs, *pieces, ring)
 
 
-def query_kernel(meta_ref, mine_ref, theirs_ref, p0, p1, p2, p3, p4, made_ref, out_ref, made_out_ref, w_ref):
+def query_kernel(meta_ref, mine_ref, theirs_ref, p0, p1, p2, p3, p4, out_ref, w_ref):
     assemble((p0, p1, p2, p3, p4), block_order(meta_ref), w_ref)
     rows = mine_ref.shape[0]
     factor = LOG2E / HD**0.5
@@ -120,31 +120,26 @@
         ).astype(jnp.bfloat16)
 
 
-def project_query(meta, mine, theirs, pieces, width, made):
+def project_query(meta, mine, theirs, pieces, width):
     rows, depth = mine.shape
     group = 4 * HD
-    anywhere = pl.BlockSpec(memory_space=pl.ANY)
     return pl.pallas_call(
         query_kernel,
-        out_shape=[
-            jax.ShapeDtypeStruct((2 * rows, width), jnp.bfloat16),
-            jax.ShapeDtypeStruct(made.shape, made.dtype),
-        ],
+        out_shape=jax.ShapeDtypeStruct((2 * rows, width), jnp.bfloat16),
         grid_spec=pltpu.PrefetchScalarGridSpec(
             num_scalar_prefetch=1,
             grid=(width // group,),
             in_specs=[pl.BlockSpec(mine.shape, lambda i, m: (0, 0))] * 2
-            + [pl.BlockSpec((p.shape[0], group), lambda i, m: (0, i)) for p in pieces]
-            + [anywhere],
-            out_specs=[pl.BlockSpec((2 * rows, group), lambda i, m: (0, i)), anywhere],
+            + [pl.BlockSpec((p.shape[0], group), lambda i, m: (0, i)) for p in pieces],
+            out_specs=pl.BlockSpec((2 * rows, group), lambda i, m: (0, i)),
             scratch_shapes=[pltpu.VMEM((depth, group), jnp.bfloat16)],
         ),
-        input_output_aliases={8: 1},
         name="project_query",
-    )(meta, mine, theirs, *pieces, made)
-
-
-def attend_kernel(meta_ref, q_ref, s2, s1, s0, c2, c1, c0, segq_ref, segk_ref, out_ref, key_ref, v_ref):
+    )(meta, mine, theirs, *pieces)
+
+
+def attend_kernel(meta_ref, q_ref, s2, s1, s0, c2, c1, c0, segq_ref, segk_ref, *refs):
+    out_ref, key_ref, v_ref = refs[-3:]
     rows, width = out_ref.shape
     span = WINDOW + BLK
     core = meta_ref[2]
@@ -195,8 +190,9 @@
     lax.fori_loop(0, blocks, block, 0)
 
 
-def attend(meta, query, width, index, same, cross, segq, segk):
+def attend(meta, query, width, index, same, cross, segq, segk, after=()):
     rows = query.shape[0]
+    tiles = rows * (WINDOW + BLK) * (width // HD)
     whole = lambda a: pl.BlockSpec(a.shape, lambda i, m: (0,) * a.ndim)
     rest = (*same, *cross, segq, segk)
     return pl.pallas_call(
@@ -205,31 +201,56 @@
         grid_spec=pltpu.PrefetchScalarGridSpec(
             num_scalar_prefetch=1,
             grid=(1,),
-            in_specs=[pl.BlockSpec((rows, width), lambda i, m: (0, index))] + [whole(a) for a in rest],
+            in_specs=[pl.BlockSpec((rows, width), lambda i, m: (0, index))] + [whole(a) for a in rest]
+            + [pl.BlockSpec(memory_space=pl.ANY)] * len(after),
             out_specs=pl.BlockSpec((rows, width), lambda i, m: (0, 0)),
             scratch_shapes=[
                 pltpu.VMEM((WINDOW + rows, HD), jnp.bfloat16),
                 pltpu.VMEM((WINDOW + rows, 2 * HD), jnp.bfloat16),
             ],
         ),
+        cost_estimate=pl.CostEstimate(
+            flops=6 * HD * tiles, transcendentals=tiles, bytes_accessed=4 * rows * width
+        ),
         name="attend",
-    )(meta, query, *rest)
+    )(meta, query, *rest, *after)
 
 
 def out_kernel(
-    meta_ref, k0, k1, g0, g1, p0, p1, p2, p3, p4, mine_ref, theirs_ref, mine_out, theirs_out, x_ref, w_ref
+    meta_ref,
+    k0,
+    k1,
+    k2,
+    g0,
+    g1,
+    g2,
+    p0,
+    p1,
+    p2,
+    p3,
+    p4,
+    mine_ref,
+    theirs_ref,
+    after_ref,
+    mine_out,
+    theirs_out,
+    x_ref,
+    w_ref,
 ):
     rows = mine_ref.shape[0]
-    group = k0.shape[1]
 
     @pl.when(pl.program_id(0) == 0)
     def _():
-        for n, ref in enumerate((k0, k1)):
-            x_ref[:, n * group : (n + 1) * group] = ref[...]
-        for n, ref in enumerate((g0, g1)):
-            columns = slice((n + 2) * group, (n + 3) * group)
-            x_ref[:rows, columns] = ref[rows:, :]
-            x_ref[rows:, columns] = ref[:rows, :]
+        start = 0
+        for ref in (k0, k1, k2):
+            stop = start + ref.shape[1]
+            x_ref[:, start:stop] = ref[...]
+            start = stop
+        for ref in (g0, g1, g2):
+            stop = start + ref.shape[1]
+            x_ref[:rows, start:stop] = ref[rows:, :]
+            x_ref[rows:, start:stop] = ref[:rows, :]
+            start = stop
 
     assemble((p0, p1, p2, p3, p4), block_order(meta_ref), w_ref, meta_ref[2] * (NY * NX // 2))
     for hidden, out, at in ((mine_ref, mine_out, 0), (theirs_ref, theirs_out, rows)):
@@ -237,7 +258,7 @@
         out[...] = (hidden[...].astype(jnp.float32) + product).astype(jnp.bfloat16)
 
 
-def project_out(meta, kept, got, pieces, mine, theirs):
+def project_out(meta, kept, got, pieces, mine, theirs, after):
     rows, width = mine.shape
     half = width // 2
     step = 256
@@ -252,7 +273,7 @@
             grid=(half // step,),
             in_specs=[whole(a) for a in (*kept, *got)]
             + [pl.BlockSpec((p.shape[0], step), lambda i, m: (0, i)) for p in pieces]
-            + [hidden, hidden],
+            + [hidden, hidden, pl.BlockSpec(memory_space=pl.ANY)],
             out_specs=[out, out],
             scratch_shapes=[
                 pltpu.VMEM((2 * rows, width), jnp.bfloat16),
@@ -260,7 +281,7 @@
             ],
         ),
         name="project_out",
-    )(meta, *kept, *got, *pieces, mine, theirs)
+    )(meta, *kept, *got, *pieces, mine, theirs, after)
 
 
 def pick_kernel(meta_ref, source_ref, a, b, c, d, after_ref, oa, ob, oc, od):
@@ -296,7 +317,7 @@
     )(meta, source_of, column, column, column, column, after)
 
 
-def own_kernel(meta_ref, source_ref, a, b, c, d, keep_ref, send_ref):
+def own_kernel(meta_ref, source_ref, a, b, c, d, after_ref, keep_ref, send_ref):
     per_chip = a.shape[0]
     y, x, core = meta_ref[0], meta_ref[1], meta_ref[2]
     refs = (a, b, c, d)
@@ -313,7 +334,7 @@
                     out_ref[i] = refs[k][at]
 
 
-def own_blocks(meta, source_of, arrived):
+def own_blocks(meta, source_of, arrived, after):
     per_chip = arrived[0].shape[0]
     shape = (per_chip // 2,) + arrived[0].shape[1:]
     whole = lambda s: pl.BlockSpec(s, lambda i, m, source_ref: (0, 0, 0))
@@ -323,11 +344,11 @@
         grid_spec=pltpu.PrefetchScalarGridSpec(
             num_scalar_prefetch=2,
             grid=(1,),
-            in_specs=[whole(a.shape) for a in arrived],
+            in_specs=[whole(a.shape) for a in arrived] + [pl.BlockSpec(memory_space=pl.ANY)],
             out_specs=[whole(shape)] * 2,
         ),
         name="own_blocks",
-    )(meta, source_of, *arrived)
+    )(meta, source_of, *arrived, after)
 
 
 def halves(part0, part1, first_core):
@@ -377,7 +398,7 @@
     same = (send_on(tail, 2, False), send_on(made, 1, False), made)
     cross = (send_on(tail, 2, True), send_on(made, 1, True), send_on(made, 0, True))
     pieces_out = ring_pieces(ring_out, 2)
-    query, made = project_query(meta, mine, theirs, pieces, half, made)
+    query = project_query(meta, mine, theirs, pieces, half)
 
     seg_pad = jnp.concatenate([jnp.full((WINDOW,), -1, jnp.int32), seg_ids])
     seg_here = lax.dynamic_slice_in_dim(seg_pad, chip * chip_rows, WINDOW + chip_rows, 0)
@@ -385,24 +406,30 @@
     segq = seg_here[WINDOW:].reshape(blocks, BLK, 1)
     segk = jnp.stack([seg_here[b * BLK : b * BLK + WINDOW + BLK] for b in range(blocks)])[:, None, :]
 
-    group = 4 * HD
-    kept = [attend(meta, query, group, i, same, cross, segq, segk) for i in range(half // group)]
-    got = [other_core(a) for a in kept]
-    out_mine, out_theirs = project_out(meta, kept, got, pieces_out, hidden_in, hidden_theirs)
-    out_got = other_core(out_theirs)
-    hidden_out = jnp.concatenate(
-        [jnp.where(first_core, out_mine, out_got), jnp.where(first_core, out_got, out_mine)], axis=1
-    )
-
     made = made.reshape(blocks, BLK, HD)
     column = jnp.concatenate([made, turn(made, "y", 1), turn(made, "y", -1), turn(made, "y", 2)], axis=0)
     total = cache_slot.shape[0]
     ids = jnp.arange(total, dtype=jnp.int32)
     source_of = jnp.sum(jnp.where(cache_slot[None, :] == ids[:, None], ids[None, :], 0), axis=1)
-    here, right, left, across = pick_blocks(meta, source_of, column, blocks, kept[0])
+
+    group = 4 * HD
+    first = attend(meta, query, group, 0, same, cross, segq, segk)
+    here, right, left, across = pick_blocks(meta, source_of, column, blocks, first)
+    second = attend(meta, query, group // 2, 2, same, cross, segq, segk, (here, *pieces_out[1:3]))
     arrived = (here, turn(right, "x", 1), turn(left, "x", -1), turn(across, "x", 2))
-    cache_keep, cache_send = own_blocks(meta, source_of, arrived)
+    cache_keep, cache_send = own_blocks(meta, source_of, arrived, second)
     cache_got = other_core(cache_send)
+
+    third = attend(meta, query, group // 2, 3, same, cross, segq, segk, (cache_send, *pieces_out[3:]))
+    kept = [first, second, third]
+    got = [other_core(a) for a in kept]
+    out_mine, out_theirs = project_out(
+        meta, kept, got, pieces_out, hidden_in, hidden_theirs, cache_send
+    )
+    out_got = other_core(out_theirs)
+    hidden_out = jnp.concatenate(
+        [jnp.where(first_core, out_mine, out_got), jnp.where(first_core, out_got, out_mine)], axis=1
+    )
     kv_cache = jnp.concatenate(
         [jnp.where(first_core, cache_keep, cache_got), jnp.where(first_core, cache_got, cache_keep)], axis=2
     ).reshape(row_count, 2 * HD)

time: 175 us -> 167 us (0.954)
  starting transfers between devices: 60.9 us -> 47.6 us
  Pallas kernels: 52.6 us -> 58.6 us
  local copies, waits for them, and re-layouts: 13.7 us -> 11.3 us
    ppermute x16, starting transfers between devices: 27.5 us -> 16.6 us  [hop(): return lax.ppermute(array, SEQ, pairs)]
    ppermute x6, waiting for transfers between devices: 9.47 us -> 2.6 us  [turn(): return lax.ppermute(array, axis, [(i, (i + by) % n) for i in range(n)])]
    ppermute x6, starting transfers between devices: 10.3 us -> 4.11 us  [turn(): return lax.ppermute(array, axis, [(i, (i + by) % n) for i in range(n)])]
    pallas_call x2 -> x3, Pallas kernels: 22.9 us -> 28.6 us  [attend(): pl.pallas_call(attend_kernel, out_shape=jax.ShapeDtypeStruct((rows, width...]
    ppermute x16, waiting for transfers between devices: 20.5 us -> 23.9 us  [hop(): return lax.ppermute(array, SEQ, pairs)]
    unnamed x61 -> x60, local copies, waits for them, and re-layouts: 9.1 us -> 5.85 us
    ppermute x5, starting transfers between devices: 14.3 us -> 17.1 us  [send_on(): return lax.ppermute(array, SEQ, pairs)]
    ppermute x5, waiting for transfers between devices: 0.01 us -> 2.69 us  [send_on(): return lax.ppermute(array, SEQ, pairs)]
  transfers between devices with their start and end apart: 34 -> 35, of which waited for: 11 -> 11; matrix products, arithmetic and copies ran while one was open for 12% -> 11% of each run, Pallas kernels for 28% -> 27%
where the time goes in v3:
time: 167 us; the launch traced here: 166 us
  Pallas kernels  58.6 us (35%)
  starting transfers between devices  47.6 us (29%)
  waiting for transfers between devices  32.7 us (20%)
  other arithmetic  14.5 us (9%)
  local copies, waits for them, and re-layouts  11.3 us (7%)
    pallas_call x3, Pallas kernels, attend(): pl.pallas_call(attend_kernel, out_shape=jax.ShapeDtypeStruct((rows, width...  28.6 us
    ppermute x16, waiting for transfers between devices, hop(): return lax.ppermute(array, SEQ, pairs)  23.9 us
    ppermute x5, starting transfers between devices, send_on(): return lax.ppermute(array, SEQ, pairs)  17.1 us
    ppermute x16, starting transfers between devices, hop(): return lax.ppermute(array, SEQ, pairs)  16.6 us
    ppermute x8, starting transfers between devices, other_core(): return lax.ppermute(array, 'core', [(0, 1), (1, 0)])  9.72 us
    pallas_call x1, Pallas kernels, project_out(): pl.pallas_call(out_kernel, out_shape=[jax.ShapeDtypeStruct((rows, half),...  9.42 us
    pallas_call x1, Pallas kernels, project_query(): pl.pallas_call(query_kernel, out_shape=jax.ShapeDtypeStruct((2 * rows, wi...  8.28 us
    unnamed x60, local copies, waits for them, and re-layouts  5.85 us
  transfers between devices with their start and end apart: 35, of which 11 were waited for; matrix products, arithmetic and copies ran while one was open for 11% of the time, Pallas kernels for 27%

profile of v3, /device:TPU:1, one launch (start us, length us, event | category | flops | bytes accessed | tf_op | source)
XLA Modules:
  0.0 165.7 jit_solution(4476767702921871514)
XLA Ops:
  1.7 3.3 %collective-permute-start.10 = (bf16[64,1024]{1,0:T(8,128)(2,1)S(1)}, bf16[64,1024]{1,0:T(8,128)(2,1)S(1)}, u32[]{:S(2)}, u32[]{:S(2)}) collective-permute-start(bf16[64,1024]{1,0:T(8,128)(2,1)S(1)} %broadcast_select_fusion.8), channel_id=1, source_target_pairs={{0,8},{8,0},{1,9},{9,1},{2,10},{10,2},{3,11},{11,3},{4,12},{12,4},... | collective-permute-start | bytes 393224 | tf_op jit(solution)/shard_map/ppermute | solution.py:27
  12.4 2.3 %collective-permute-start.12 = (bf16[128,1024]{1,0:T(8,128)(2,1)S(1)}, bf16[128,1024]{1,0:T(8,128)(2,1)S(1)}, u32[]{:S(2)}, u32[]{:S(2)}) collective-permute-start(bf16[128,1024]{1,0:T(8,128)(2,1)S(1)} %pad_maximum_fusion.3), channel_id=1, source_target_pairs={{0,48},{8,200},{16,0},{24,216},{32,16},{40,232},{48,32},{56,248},{... | collective-permute-start | bytes 786440 | tf_op jit(solution)/shard_map/ppermute | solution.py:43
  18.4 5.4 %collective-permute-done.4 = bf16[64,1152]{1,0:T(8,128)(2,1)S(1)} collective-permute-done((bf16[64,1152]{1,0:T(8,128)(2,1)S(1)}, bf16[64,1152]{1,0:T(8,128)(2,1)S(1)}, u32[]{:S(2)}, u32[]{:S(2)}) %collective-permute-start.4) | collective-permute-done | bytes 147488 | tf_op jit(solution)/shard_map/ppermute | solution.py:43
  23.9 2.4 %collective-permute-start.7 = (bf16[512,1152]{1,0:T(8,128)(2,1)S(1)}, bf16[512,1152]{1,0:T(8,128)(2,1)S(1)}, u32[]{:S(2)}, u32[]{:S(2)}) collective-permute-start(bf16[512,1152]{1,0:T(8,128)(2,1)S(1)} %constant_dynamic-update-slice_fusion.p0), channel_id=1, source_target_pairs={{0,192},{8,56},{16,208},{24,8},{32,224},{40,24},{48,240},{56,40},{... | collective-permute-start | bytes 3538952 | tf_op jit(solution)/shard_map/ppermute | solution.py:43
  30.0 2.3 %collective-permute-done.13 = bf16[64,1024]{1,0:T(8,128)(2,1)S(1)} collective-permute-done((bf16[64,1024]{1,0:T(8,128)(2,1)S(1)}, bf16[64,1024]{1,0:T(8,128)(2,1)S(1)}, u32[]{:S(2)}, u32[]{:S(2)}) %collective-permute-start.13) | collective-permute-done | bytes 131104 | tf_op jit(solution)/shard_map/ppermute | solution.py:43
  34.0 6.8 %collective-permute-done.7.p2 = bf16[512,1152]{1,0:T(8,128)(2,1)S(1)} collective-permute-done((bf16[512,1152]{1,0:T(8,128)(2,1)S(1)}, bf16[512,1152]{1,0:T(8,128)(2,1)S(1)}, u32[]{:S(2)}, u32[]{:S(2)}) %collective-permute-start.7) | collective-permute-done | bytes 1179680 | tf_op jit(solution)/shard_map/ppermute | solution.py:43
  41.9 3.5 %collective-permute-start.9 = (bf16[256,1152]{1,0:T(8,128)(2,1)S(1)}, bf16[256,1152]{1,0:T(8,128)(2,1)}, u32[]{:S(2)}, u32[]{:S(2)}) collective-permute-start(bf16[256,1152]{1,0:T(8,128)(2,1)S(1)} %slice.94), channel_id=1, source_target_pairs={{0,192},{8,56},{16,208},{24,8},{32,224},{40,24},{48,240},{56,40},{... | collective-permute-start | bytes 1769480 | tf_op jit(solution)/shard_map/ppermute | solution.py:43
  46.8 2.4 %fusion.5 = (bf16[384,2048]{1,0:T(8,128)(2,1)}, bf16[384,2048]{1,0:T(8,128)(2,1)}) fusion(bf16[384,2048]{1,0:T(8,128)(2,1)S(1)} %collective-permute-done.theirs_ref, f32[384]{0:T(512)S(1)} %add_rsqrt_fusion, f32[2048]{0:T(1024)S(1)} %convert_element_type.17, f32[384]{0:T(512)S(1)} %add_rsqrt_fusion.1, bf16[384,2048]{1,0:T(8,128)(2,1)S(1)} %copy-done), kind=kLoop, calls=%fused_computation.9 | loop fusion | flops 6291456 | bytes 6302720 | tf_op jit(solution)/shard_map/convert_element_type | solution.py:23
  49.3 3.0 %collective-permute-done.9.p4 = bf16[256,1152]{1,0:T(8,128)(2,1)} collective-permute-done((bf16[256,1152]{1,0:T(8,128)(2,1)S(1)}, bf16[256,1152]{1,0:T(8,128)(2,1)}, u32[]{:S(2)}, u32[]{:S(2)}) %collective-permute-start.9) | collective-permute-done | bytes 589856 | tf_op jit(solution)/shard_map/ppermute | solution.py:43
  52.3 4.9 %collective-permute-done.8.p3 = bf16[256,1152]{1,0:T(8,128)(2,1)} collective-permute-done((bf16[256,1152]{1,0:T(8,128)(2,1)S(1)}, bf16[256,1152]{1,0:T(8,128)(2,1)}, u32[]{:S(2)}, u32[]{:S(2)}) %collective-permute-start.8) | collective-permute-done | bytes 589856 | tf_op jit(solution)/shard_map/ppermute | solution.py:43
  57.1 4.6 %project_kv.1 = (bf16[768,128]{1,0:T(8,128)(2,1)}, bf16[512,1024]{1,0:T(8,128)(2,1)}) custom-call(s32[3]{0:T(128)} %pad_add_fusion.meta_ref, bf16[384,2048]{1,0:T(8,128)(2,1)} %get-tuple-element.43.mine_ref, bf16[384,2048]{1,0:T(8,128)(2,1)} %get-tuple-element.42.theirs_ref, bf16[512,1152]{1,0:T(8,128)(2,1)} %copy-done.6, ...), custom_call_target="tpu_custom_call", output_to_operand_aliasing={{1}: (8, {})} | custom-call | tf_op jit(solution)/shard_map/project_kv/pallas_call | solution.py:93
  64.0 4.8 %collective-permute-start.17 = (bf16[256,128]{1,0:T(8,128)(2,1)S(1)}, bf16[256,128]{1,0:T(8,128)(2,1)S(1)}, u32[]{:S(2)}, u32[]{:S(2)}) collective-permute-start(bf16[256,128]{1,0:T(8,128)(2,1)S(1)} %slice.80), channel_id=1, source_target_pairs={{0,40},{8,32},{16,56},{24,48},{32,72},{40,64},{48,88},{56,80},{64,... | collective-permute-start | bytes 196616 | tf_op jit(solution)/shard_map/ppermute | solution.py:369
  68.8 4.8 %collective-permute-start.15 = (bf16[256,128]{1,0:T(8,128)(2,1)S(1)}, bf16[256,128]{1,0:T(8,128)(2,1)S(1)}, u32[]{:S(2)}, u32[]{:S(2)}) collective-permute-start(bf16[256,128]{1,0:T(8,128)(2,1)S(1)} %slice.80), channel_id=1, source_target_pairs={{0,32},{8,40},{16,48},{24,56},{32,64},{40,72},{48,80},{56,88},{64,... | collective-permute-start | bytes 196616 | tf_op jit(solution)/shard_map/ppermute | solution.py:369
  74.5 2.7 %collective-permute-done.17.c2 = bf16[256,128]{1,0:T(8,128)(2,1)S(1)} collective-permute-done((bf16[256,128]{1,0:T(8,128)(2,1)S(1)}, bf16[256,128]{1,0:T(8,128)(2,1)S(1)}, u32[]{:S(2)}, u32[]{:S(2)}) %collective-permute-start.17) | collective-permute-done | bytes 65568 | tf_op jit(solution)/shard_map/ppermute | solution.py:369
  78.5 6.2 %collective-permute-start.16 = (bf16[768,128]{1,0:T(8,128)(2,1)}, bf16[768,128]{1,0:T(8,128)(2,1)S(1)}, u32[]{:S(2)}, u32[]{:S(2)}) collective-permute-start(bf16[768,128]{1,0:T(8,128)(2,1)} %get-tuple-element.12.s0), channel_id=1, source_target_pairs={{0,16},{8,24},{16,32},{24,40},{32,48},{40,56},{48,64},{56,72},{64,... | collective-permute-start | bytes 589832 | tf_op jit(solution)/shard_map/ppermute | solution.py:369
  86.5 8.3 %project_query.1.q_ref = bf16[768,1024]{1,0:T(8,128)(2,1)} custom-call(s32[3]{0:T(128)} %pad_add_fusion.meta_ref, bf16[384,2048]{1,0:T(8,128)(2,1)} %get-tuple-element.43.mine_ref, bf16[384,2048]{1,0:T(8,128)(2,1)} %get-tuple-element.42.theirs_ref, bf16[512,1152]{1,0:T(8,128)(2,1)} %copy-done.6, bf16[512,1152]{1,0:T(8,128)(2,1)} %copy-done.3, ...), custom_call_target="tpu_custom_call" | custom-call | tf_op jit(solution)/shard_map/project_query/pallas_call | solution.py:126
  96.5 11.5 %attend.3.after_ref.k0 = bf16[768,512]{1,0:T(8,128)(2,1)} custom-call(s32[3]{0:T(128)} %pad_add_fusion.meta_ref, bf16[768,1024]{1,0:T(8,128)(2,1)} %project_query.1.q_ref, bf16[256,128]{1,0:T(8,128)(2,1)} %copy-done.24, bf16[768,128]{1,0:T(8,128)(2,1)} %copy-done.14, bf16[768,128]{1,0:T(8,128)(2,1)} %get-tuple-element.12.s0, bf16[256,128]{1,0:T(8,128)(2,1)} %copy-done.23, ...), custom_call_target="tpu_custom_call" | custom-call | flops 2717908992 | bytes 1572864 | tf_op jit(solution)/shard_map/attend/pallas_call | solution.py:198
  112.4 5.1 %pick_blocks.1 = (bf16[6,128,128]{2,1,0:T(8,128)(2,1)}, bf16[6,128,128]{2,1,0:T(8,128)(2,1)}, bf16[6,128,128]{2,1,0:T(8,128)(2,1)}, bf16[6,128,128]{2,1,0:T(8,128)(2,1)}) custom-call(s32[3]{0:T(128)} %pad_add_fusion.meta_ref, s32[96]{0:T(128)} %select_reduce_fusion.source_ref, bf16[24,128,128]{2,1,0:T(8,128)(2,1)} %pad_maximum_fusion.1.a.b.c.d, ...), custom_call_target="tpu_custom_call" | custom-call | tf_op jit(solution)/shard_map/pick_blocks/pallas_call | solution.py:307
  121.6 2.6 %collective-permute-done.25.b = bf16[6,128,128]{2,1,0:T(8,128)(2,1)S(1)} collective-permute-done((bf16[6,128,128]{2,1,0:T(8,128)(2,1)}, bf16[6,128,128]{2,1,0:T(8,128)(2,1)S(1)}, u32[]{:S(2)}, u32[]{:S(2)}) %collective-permute-start.25) | collective-permute-done | bytes 196640 | tf_op jit(solution)/shard_map/ppermute | solution.py:32
  124.4 8.6 %attend.4.after_ref.k1 = bf16[768,256]{1,0:T(8,128)(2,1)} custom-call(s32[3]{0:T(128)} %pad_add_fusion.meta_ref, bf16[768,1024]{1,0:T(8,128)(2,1)} %project_query.1.q_ref, bf16[256,128]{1,0:T(8,128)(2,1)} %copy-done.24, bf16[768,128]{1,0:T(8,128)(2,1)} %copy-done.14, bf16[768,128]{1,0:T(8,128)(2,1)} %get-tuple-element.12.s0, bf16[256,128]{1,0:T(8,128)(2,1)} %copy-done.23, ...), custom_call_target="tpu_custom_call" | custom-call | flops 1358954496 | bytes 786432 | tf_op jit(solution)/shard_map/attend/pallas_call | solution.py:198
  133.0 2.8 %collective-permute-start.31 = (bf16[768,256]{1,0:T(8,128)(2,1)}, bf16[768,256]{1,0:T(8,128)(2,1)S(1)}, u32[]{:S(2)}, u32[]{:S(2)}) collective-permute-start(bf16[768,256]{1,0:T(8,128)(2,1)} %attend.4.after_ref.k1), channel_id=1, source_target_pairs={{0,8},{8,0},{1,9},{9,1},{2,10},{10,2},{3,11},{11,3},{4,12},{12,4},... | collective-permute-start | bytes 1179656 | tf_op jit(solution)/shard_map/ppermute | solution.py:27
  136.4 2.7 %own_blocks.1 = (bf16[3,128,128]{2,1,0:T(8,128)(2,1)}, bf16[3,128,128]{2,1,0:T(8,128)(2,1)}) custom-call(s32[3]{0:T(128)} %pad_add_fusion.meta_ref, s32[96]{0:T(128)} %select_reduce_fusion.source_ref, bf16[6,128,128]{2,1,0:T(8,128)(2,1)} %get-tuple-element.13.refs_0_.a, bf16[6,128,128]{2,1,0:T(8,128)(2,1)} %copy-done.16, bf16[6,128,128]{2,1,0:T(8,128)(2,1)} %copy-done.17, ...), custom_call_target="tpu_custom_call" | custom-call | tf_op jit(solution)/shard_map/own_blocks/pallas_call | solution.py:341
  139.1 8.5 %attend.5.k2 = bf16[768,256]{1,0:T(8,128)(2,1)} custom-call(s32[3]{0:T(128)} %pad_add_fusion.meta_ref, bf16[768,1024]{1,0:T(8,128)(2,1)} %project_query.1.q_ref, bf16[256,128]{1,0:T(8,128)(2,1)} %copy-done.24, bf16[768,128]{1,0:T(8,128)(2,1)} %copy-done.14, bf16[768,128]{1,0:T(8,128)(2,1)} %get-tuple-element.12.s0, bf16[256,128]{1,0:T(8,128)(2,1)} %copy-done.23, ...), custom_call_target="tpu_custom_call" | custom-call | flops 1358954496 | bytes 786432 | tf_op jit(solution)/shard_map/attend/pallas_call | solution.py:198
  150.6 9.4 %project_out.1 = (bf16[384,1024]{1,0:T(8,128)(2,1)}, bf16[384,1024]{1,0:T(8,128)(2,1)}) custom-call(s32[3]{0:T(128)} %pad_add_fusion.meta_ref, bf16[768,512]{1,0:T(8,128)(2,1)} %attend.3.after_ref.k0, bf16[768,256]{1,0:T(8,128)(2,1)} %attend.4.after_ref.k1, bf16[768,256]{1,0:T(8,128)(2,1)} %attend.5.k2, bf16[768,512]{1,0:T(8,128)(2,1)} %copy-done.9, ...), custom_call_target="tpu_custom_call" | custom-call | tf_op jit(solution)/shard_map/project_out/pallas_call | solution.py:268
  (158 shorter events, 46.0 us)
Async XLA Ops:
  6.9 26.7 %collective-permute-start = (bf16[384,2048]{1,0:T(8,128)(2,1)}, bf16[384,2048]{1,0:T(8,128)(2,1)S(1)}, u32[]{:S(2)}, u32[]{:S(2)}) collective-permute-start(bf16[384,2048]{1,0:T(8,128)(2,1)} %mine_ref.1), channel_id=1, source_target_pairs={{0,8},{8,0},{1,9},{9,1},{2,10},{10,2},{3,11},{11,3},{4,12},{12,4},... | collective-permute-start | bytes 4718600 | tf_op jit(solution)/shard_map/ppermute | solution.py:27
  12.4 14.5 %collective-permute-start.12 = (bf16[128,1024]{1,0:T(8,128)(2,1)S(1)}, bf16[128,1024]{1,0:T(8,128)(2,1)S(1)}, u32[]{:S(2)}, u32[]{:S(2)}) collective-permute-start(bf16[128,1024]{1,0:T(8,128)(2,1)S(1)} %pad_maximum_fusion.3), channel_id=1, source_target_pairs={{0,48},{8,200},{16,0},{24,216},{32,16},{40,232},{48,32},{56,248},{... | collective-permute-start | bytes 786440 | tf_op jit(solution)/shard_map/ppermute | solution.py:43
  14.7 12.5 %collective-permute-start.11 = (bf16[128,1024]{1,0:T(8,128)(2,1)S(1)}, bf16[128,1024]{1,0:T(8,128)(2,1)S(1)}, u32[]{:S(2)}, u32[]{:S(2)}) collective-permute-start(bf16[128,1024]{1,0:T(8,128)(2,1)S(1)} %pad_maximum_fusion.3), channel_id=1, source_target_pairs={{0,16},{8,72},{16,32},{24,88},{32,48},{40,104},{48,0},{56,120},{64... | collective-permute-start | bytes 786440 | tf_op jit(solution)/shard_map/ppermute | solution.py:43
  16.1 7.8 %collective-permute-start.5 = (bf16[64,1152]{1,0:T(8,128)(2,1)S(1)}, bf16[64,1152]{1,0:T(8,128)(2,1)S(1)}, u32[]{:S(2)}, u32[]{:S(2)}) collective-permute-start(bf16[64,1152]{1,0:T(8,128)(2,1)S(1)} %slice.92), channel_id=1, source_target_pairs={{0,48},{8,200},{16,0},{24,216},{32,16},{40,232},{48,32},{56,248},{... | collective-permute-start | bytes 442376 | tf_op jit(solution)/shard_map/ppermute | solution.py:43
  23.9 16.9 %collective-permute-start.7 = (bf16[512,1152]{1,0:T(8,128)(2,1)S(1)}, bf16[512,1152]{1,0:T(8,128)(2,1)S(1)}, u32[]{:S(2)}, u32[]{:S(2)}) collective-permute-start(bf16[512,1152]{1,0:T(8,128)(2,1)S(1)} %constant_dynamic-update-slice_fusion.p0), channel_id=1, source_target_pairs={{0,192},{8,56},{16,208},{24,8},{32,224},{40,24},{48,240},{56,40},{... | collective-permute-start | bytes 3538952 | tf_op jit(solution)/shard_map/ppermute | solution.py:43
  26.3 19.2 %collective-permute-start.6 = (bf16[512,1152]{1,0:T(8,128)(2,1)S(1)}, bf16[512,1152]{1,0:T(8,128)(2,1)S(1)}, u32[]{:S(2)}, u32[]{:S(2)}) collective-permute-start(bf16[512,1152]{1,0:T(8,128)(2,1)S(1)} %constant_dynamic-update-slice_fusion.p0), channel_id=1, source_target_pairs={{0,64},{8,24},{16,80},{24,40},{32,96},{40,56},{48,112},{56,8},{64,... | collective-permute-start | bytes 3538952 | tf_op jit(solution)/shard_map/ppermute | solution.py:43
  41.9 10.3 %collective-permute-start.9 = (bf16[256,1152]{1,0:T(8,128)(2,1)S(1)}, bf16[256,1152]{1,0:T(8,128)(2,1)}, u32[]{:S(2)}, u32[]{:S(2)}) collective-permute-start(bf16[256,1152]{1,0:T(8,128)(2,1)S(1)} %slice.94), channel_id=1, source_target_pairs={{0,192},{8,56},{16,208},{24,8},{32,224},{40,24},{48,240},{56,40},{... | collective-permute-start | bytes 1769480 | tf_op jit(solution)/shard_map/ppermute | solution.py:43
  46.5 10.6 %collective-permute-start.8 = (bf16[256,1152]{1,0:T(8,128)(2,1)S(1)}, bf16[256,1152]{1,0:T(8,128)(2,1)}, u32[]{:S(2)}, u32[]{:S(2)}) collective-permute-start(bf16[256,1152]{1,0:T(8,128)(2,1)S(1)} %slice.93), channel_id=1, source_target_pairs={{0,64},{8,24},{16,80},{24,40},{32,96},{40,56},{48,112},{56,8},{64,... | collective-permute-start | bytes 1769480 | tf_op jit(solution)/shard_map/ppermute | solution.py:43
  61.7 46.3 %collective-permute-start.24 = (bf16[512,1024]{1,0:T(8,128)(2,1)}, bf16[512,1024]{1,0:T(8,128)(2,1)S(1)}, u32[]{:S(2)}, u32[]{:S(2)}) collective-permute-start(bf16[512,1024]{1,0:T(8,128)(2,1)} %get-tuple-element.14.p0), channel_id=1, source_target_pairs={{0,192},{8,56},{16,208},{24,8},{32,224},{40,24},{48,240},{56,40},{... | collective-permute-start | bytes 3145736 | tf_op jit(solution)/shard_map/ppermute | solution.py:43
  61.7 46.9 %collective-permute-start.23 = (bf16[512,1024]{1,0:T(8,128)(2,1)}, bf16[512,1024]{1,0:T(8,128)(2,1)S(1)}, u32[]{:S(2)}, u32[]{:S(2)}) collective-permute-start(bf16[512,1024]{1,0:T(8,128)(2,1)} %get-tuple-element.14.p0), channel_id=1, source_target_pairs={{0,64},{8,24},{16,80},{24,40},{32,96},{40,56},{48,112},{56,8},{64,... | collective-permute-start | bytes 3145736 | tf_op jit(solution)/shard_map/ppermute | solution.py:43
  64.0 13.2 %collective-permute-start.17 = (bf16[256,128]{1,0:T(8,128)(2,1)S(1)}, bf16[256,128]{1,0:T(8,128)(2,1)S(1)}, u32[]{:S(2)}, u32[]{:S(2)}) collective-permute-start(bf16[256,128]{1,0:T(8,128)(2,1)S(1)} %slice.80), channel_id=1, source_target_pairs={{0,40},{8,32},{16,56},{24,48},{32,72},{40,64},{48,88},{56,80},{64,... | collective-permute-start | bytes 196616 | tf_op jit(solution)/shard_map/ppermute | solution.py:369
  68.8 9.7 %collective-permute-start.15 = (bf16[256,128]{1,0:T(8,128)(2,1)S(1)}, bf16[256,128]{1,0:T(8,128)(2,1)S(1)}, u32[]{:S(2)}, u32[]{:S(2)}) collective-permute-start(bf16[256,128]{1,0:T(8,128)(2,1)S(1)} %slice.80), channel_id=1, source_target_pairs={{0,32},{8,40},{16,48},{24,56},{32,64},{40,72},{48,80},{56,88},{64,... | collective-permute-start | bytes 196616 | tf_op jit(solution)/shard_map/ppermute | solution.py:369
  74.5 20.2 %collective-permute-start.19 = (bf16[768,128]{1,0:T(8,128)(2,1)}, bf16[768,128]{1,0:T(8,128)(2,1)S(1)}, u32[]{:S(2)}, u32[]{:S(2)}) collective-permute-start(bf16[768,128]{1,0:T(8,128)(2,1)} %get-tuple-element.12.s0), channel_id=1, source_target_pairs={{0,8},{8,0},{16,24},{24,16},{32,40},{40,32},{48,56},{56,48},{64,72... | collective-permute-start | bytes 589832 | tf_op jit(solution)/shard_map/ppermute | solution.py:369
  77.2 17.7 %collective-permute-start.18 = (bf16[768,128]{1,0:T(8,128)(2,1)}, bf16[768,128]{1,0:T(8,128)(2,1)S(1)}, u32[]{:S(2)}, u32[]{:S(2)}) collective-permute-start(bf16[768,128]{1,0:T(8,128)(2,1)} %get-tuple-element.12.s0), channel_id=1, source_target_pairs={{0,24},{8,16},{16,40},{24,32},{32,56},{40,48},{48,72},{56,64},{64,... | collective-permute-start | bytes 589832 | tf_op jit(solution)/shard_map/ppermute | solution.py:369
  78.5 17.2 %collective-permute-start.16 = (bf16[768,128]{1,0:T(8,128)(2,1)}, bf16[768,128]{1,0:T(8,128)(2,1)S(1)}, u32[]{:S(2)}, u32[]{:S(2)}) collective-permute-start(bf16[768,128]{1,0:T(8,128)(2,1)} %get-tuple-element.12.s0), channel_id=1, source_target_pairs={{0,16},{8,24},{16,32},{24,40},{32,48},{40,56},{48,64},{56,72},{64,... | collective-permute-start | bytes 589832 | tf_op jit(solution)/shard_map/ppermute | solution.py:369
  94.8 15.7 %collective-permute-start.22 = (bf16[6,128,128]{2,1,0:T(8,128)(2,1)}, bf16[6,128,128]{2,1,0:T(8,128)(2,1)S(1)}, u32[]{:S(2)}, u32[]{:S(2)}) collective-permute-start(bf16[6,128,128]{2,1,0:T(8,128)(2,1)} %bitcast.4), channel_id=1, source_target_pairs={{0,128},{64,192},{128,0},{192,64},{1,129},{65,193},{129,1},{193,65... | collective-permute-start | bytes 589832 | tf_op jit(solution)/shard_map/ppermute | solution.py:32
  94.9 15.6 %collective-permute-start.21 = (bf16[6,128,128]{2,1,0:T(8,128)(2,1)}, bf16[6,128,128]{2,1,0:T(8,128)(2,1)S(1)}, u32[]{:S(2)}, u32[]{:S(2)}) collective-permute-start(bf16[6,128,128]{2,1,0:T(8,128)(2,1)} %bitcast.4), channel_id=1, source_target_pairs={{0,192},{64,0},{128,64},{192,128},{1,193},{65,1},{129,65},{193,129... | collective-permute-start | bytes 589832 | tf_op jit(solution)/shard_map/ppermute | solution.py:32
  95.8 14.7 %collective-permute-start.20 = (bf16[6,128,128]{2,1,0:T(8,128)(2,1)}, bf16[6,128,128]{2,1,0:T(8,128)(2,1)S(1)}, u32[]{:S(2)}, u32[]{:S(2)}) collective-permute-start(bf16[6,128,128]{2,1,0:T(8,128)(2,1)} %bitcast.4), channel_id=1, source_target_pairs={{0,64},{64,128},{128,192},{192,0},{1,65},{65,129},{129,193},{193,1... | collective-permute-start | bytes 589832 | tf_op jit(solution)/shard_map/ppermute | solution.py:32
  108.0 31.1 %collective-permute-start.29 = (bf16[256,1024]{1,0:T(8,128)(2,1)S(1)}, bf16[256,1024]{1,0:T(8,128)(2,1)}, u32[]{:S(2)}, u32[]{:S(2)}) collective-permute-start(bf16[256,1024]{1,0:T(8,128)(2,1)S(1)} %slice.98), channel_id=1, source_target_pairs={{0,192},{8,56},{16,208},{24,8},{32,224},{40,24},{48,240},{56,40},{... | collective-permute-start | bytes 1572872 | tf_op jit(solution)/shard_map/ppermute | solution.py:43
  109.5 29.6 %collective-permute-start.28 = (bf16[256,1024]{1,0:T(8,128)(2,1)}, bf16[256,1024]{1,0:T(8,128)(2,1)}, u32[]{:S(2)}, u32[]{:S(2)}) collective-permute-start(bf16[256,1024]{1,0:T(8,128)(2,1)} %slice.97), channel_id=1, source_target_pairs={{0,64},{8,24},{16,80},{24,40},{32,96},{40,56},{48,112},{56,8},{64,... | collective-permute-start | bytes 1572872 | tf_op jit(solution)/shard_map/ppermute | solution.py:43
  118.2 30.0 %collective-permute-start.30 = (bf16[768,512]{1,0:T(8,128)(2,1)S(1)}, bf16[768,512]{1,0:T(8,128)(2,1)S(1)}, u32[]{:S(2)}, u32[]{:S(2)}) collective-permute-start(bf16[768,512]{1,0:T(8,128)(2,1)S(1)} %copy-done.7), channel_id=1, source_target_pairs={{0,8},{8,0},{1,9},{9,1},{2,10},{10,2},{3,11},{11,3},{4,12},{12,4},... | collective-permute-start | bytes 2359304 | tf_op jit(solution)/shard_map/ppermute | solution.py:27
  120.0 12.9 %collective-permute-start.26 = (bf16[6,128,128]{2,1,0:T(8,128)(2,1)}, bf16[6,128,128]{2,1,0:T(8,128)(2,1)S(1)}, u32[]{:S(2)}, u32[]{:S(2)}) collective-permute-start(bf16[6,128,128]{2,1,0:T(8,128)(2,1)} %get-tuple-element.16), channel_id=1, source_target_pairs={{0,48},{16,0},{32,16},{48,32},{1,49},{17,1},{33,17},{49,33},{2,50}... | collective-permute-start | bytes 589832 | tf_op jit(solution)/shard_map/ppermute | solution.py:32
  124.2 11.5 %collective-permute-start.27 = (bf16[6,128,128]{2,1,0:T(8,128)(2,1)}, bf16[6,128,128]{2,1,0:T(8,128)(2,1)S(1)}, u32[]{:S(2)}, u32[]{:S(2)}) collective-permute-start(bf16[6,128,128]{2,1,0:T(8,128)(2,1)} %get-tuple-element.17), channel_id=1, source_target_pairs={{0,32},{16,48},{32,0},{48,16},{1,33},{17,49},{33,1},{49,17},{2,34}... | collective-permute-start | bytes 589832 | tf_op jit(solution)/shard_map/ppermute | solution.py:32
  133.0 15.3 %collective-permute-start.31 = (bf16[768,256]{1,0:T(8,128)(2,1)}, bf16[768,256]{1,0:T(8,128)(2,1)S(1)}, u32[]{:S(2)}, u32[]{:S(2)}) collective-permute-start(bf16[768,256]{1,0:T(8,128)(2,1)} %attend.4.after_ref.k1), channel_id=1, source_target_pairs={{0,8},{8,0},{1,9},{9,1},{2,10},{10,2},{3,11},{11,3},{4,12},{12,4},... | collective-permute-start | bytes 1179656 | tf_op jit(solution)/shard_map/ppermute | solution.py:27
  (38 other events, 278.1 us)
